TPU v7x, 256 devices: a whole 4x4x8 slice. The times are simulated.
256 devices in a mesh: req: 64 (over z, x, core), ffn: 4 (over y).
Axes of the slice: x: 4, y: 4, z: 8, core: 2. Of those that a mesh axis runs over, the one named last changes fastest.
Arguments:
- residual: bfloat16 [16384, 2048], P('req')
- queries: bfloat16 [16384, 4096], P('req', 'ffn')
- rotated_key_rows: bfloat16 [16384, 2048], P('req', 'ffn')
- values: bfloat16 [16384, 2048], P('req', 'ffn'), may hold values from -6 to 6
- req_start: int32 [16384], P('req'), may hold values from 0 to 16383, as said below
- head_sink_logit: float32 [32], P('ffn'), may hold values from 6 to 11
- out_proj: bfloat16 [4096, 2048], P('ffn', 'req'), may hold values from -0.25 to 0.25
- mid_gain: float32 [2048], replicated, may hold values from 0.1 to 1.9
- router_logits: float32 [16384, 8], P('req')
- routes: int32 [16384, 2], P('req'), may hold values from 0 to 63, as said below
- placement: int32 [64], replicated, may hold values from 0 to 7, as said below
- w_gate: bfloat16 [64, 2048, 3072], P('req', None, 'ffn'), as said below
- w_up: bfloat16 [64, 2048, 3072], P('req', None, 'ffn'), as said below
- w_down: bfloat16 [64, 2048, 3072], P('req', None, 'ffn'), as said below
Outputs:
- layer_out: bfloat16 [16384, 2048], P('req', 'ffn')
Inputs may be any that keep to these rules, and one draw needn't show every extreme that they name: req_start[p] is the first position of the request that holds position p; requests are runs of consecutive positions, each at most 8192 long, one is exactly 8192 long, and the last position is a request of one token. `routes`: the two entries of a token name indices that host different experts. Among the 512 entries of the tokens of one index of req, an index appears at most 10 times, and every index that hosts one certain expert appears exactly 10 times, in every such block. `placement`: every expert is hosted at one index or more. `w_gate`: rows k and m are equal where placement[k] == placement[m]. `w_up`: rows k and m are equal where placement[k] == placement[m]. `w_down`: rows k and m are equal where placement[k] == placement[m].
All inputs are finite; a program needn't handle non-finite values.
Results may differ from a plain program's by a relative error of at most 0.0075.
Values may be sent and summed in bfloat16 or wider, within the bound.
A program may use at most 128 MiB of HBM per device.

v0:
```python
import jax
import jax.numpy as jnp
from jax import lax
from jax.sharding import PartitionSpec as P

QUERY_HEADS = 32
KEY_VALUE_HEADS = 16
HEAD_SIZE = 128
EXPERTS = 8


EPS = 1e-06


def shifted(value, axis, steps):
    count = lax.axis_size(axis)
    initial, last = (max(0, -steps), min(count, count - steps))
    return lax.ppermute(value, axis, [(source, source + steps) for source in range(initial, last)])


def step_back(keys_in_block, values_in_block):
    return shifted((keys_in_block, values_in_block), "req", 1)


def per_device(
    residual,
    queries,
    rotated_key_rows,
    values,
    req_start,
    head_sink_logit,
    out_proj,
    mid_gain,
    router_logits,
    routes,
    placement,
    w_gate,
    w_up,
    w_down,
):
    tok_count = residual.shape[0]
    model_width = residual.shape[1]
    req_size = lax.axis_size("req")
    ffn_size = lax.axis_size("ffn")
    own_req = lax.axis_index("req")
    own_ffn = lax.axis_index("ffn")
    query_group_width = QUERY_HEADS // KEY_VALUE_HEADS
    kv_heads = rotated_key_rows.shape[1] // HEAD_SIZE
    quarter = model_width // ffn_size
    gate_mat = w_gate[0]
    up_mat = w_up[0]
    down_mat = w_down[0]
    shard_queries = queries.reshape(tok_count, kv_heads, query_group_width, HEAD_SIZE)
    local_keys = rotated_key_rows.reshape(tok_count, kv_heads, HEAD_SIZE)
    local_values = values.reshape(tok_count, kv_heads, HEAD_SIZE)
    win_span = min(16, req_size // 2)
    window = win_span * tok_count
    query_pos = own_req * tok_count + jnp.arange(tok_count, dtype=jnp.int32)
    logit_scale_factor = HEAD_SIZE ** (-0.5)

    def attend(carry_state, keys_in_block, values_in_block, key_first):
        running_max, row_total, weighted_value_sum = carry_state
        attention_logits = (
            jnp.einsum(
                "veck,uek->ecvu", shard_queries, keys_in_block, preferred_element_type=jnp.float32
            )
            * logit_scale_factor
        )
        key_pos = key_first + jnp.arange(keys_in_block.shape[0], dtype=jnp.int32)
        visible = (
            (key_pos[None, :] >= req_start[:, None])
            & (key_pos[None, :] <= query_pos[:, None])
            & (query_pos[:, None] - key_pos[None, :] < window)
        )
        attention_logits = jnp.where(visible[None, None], attention_logits, -jnp.inf)
        new_max = jnp.maximum(running_max, jnp.max(attention_logits, axis=-1))
        probs = jnp.exp(attention_logits - new_max[..., None])
        factor = jnp.exp(running_max - new_max)
        row_total = row_total * factor + jnp.sum(probs, axis=-1)
        weighted_value_sum = weighted_value_sum * factor[..., None] + jnp.einsum(
            "plyw,wpj->plyj",
            probs.astype(jnp.bfloat16),
            values_in_block,
            preferred_element_type=jnp.float32,
        )
        return (new_max, row_total, weighted_value_sum)

    initial_sink_logit = jnp.broadcast_to(
        head_sink_logit.reshape(kv_heads, query_group_width, 1),
        (kv_heads, query_group_width, tok_count),
    )
    carry_state = (
        initial_sink_logit,
        jnp.ones((kv_heads, query_group_width, tok_count), jnp.float32),
        jnp.zeros((kv_heads, query_group_width, tok_count, HEAD_SIZE), jnp.float32),
    )
    carry_state = attend(carry_state, local_keys, local_values, own_req * tok_count)
    pair_count = win_span // 2

    def pair_step(step_idx, loop_carry):
        folded, near_keys, near_values = loop_carry
        mid_keys, mid_values = step_back(near_keys, near_values)
        far_keys, far_values = step_back(mid_keys, mid_values)
        key_first = (own_req - 2 * step_idx - 2) * tok_count
        folded = attend(
            folded,
            jnp.concatenate([far_keys, mid_keys], 0),
            jnp.concatenate([far_values, mid_values], 0),
            key_first,
        )
        return (folded, far_keys, far_values)

    carry_state, unused_keys, unused_values = lax.fori_loop(
        0, pair_count, pair_step, (carry_state, local_keys, local_values)
    )
    running_max, row_total, weighted_value_sum = carry_state
    attended = (weighted_value_sum / row_total[..., None]).astype(jnp.bfloat16)
    flat_attended = jnp.transpose(attended, (2, 0, 1, 3)).reshape(tok_count, -1)
    proj = jnp.dot(
        flat_attended,
        lax.all_gather(out_proj, "req", axis=1, tiled=True),
        preferred_element_type=jnp.float32,
    )
    summed = lax.psum(proj.astype(jnp.bfloat16), "ffn").astype(jnp.float32)
    hidden_state = residual.astype(jnp.float32) + summed
    mean_sq = jnp.mean(hidden_state * hidden_state, axis=1, keepdims=True)
    normed = (hidden_state * lax.rsqrt(mean_sq + EPS) * mid_gain).astype(jnp.bfloat16)
    own_hidden = lax.dynamic_slice_in_dim(hidden_state, own_ffn * quarter, quarter, 1)
    capacity = 5 * tok_count // (2 * req_size)
    flat_routes = routes.reshape(-1)
    slot_iota = jnp.arange(req_size, dtype=jnp.int32)
    dest_hot = (flat_routes[:, None] == slot_iota[None, :]).astype(jnp.int32)
    slot_depth = jnp.sum((jnp.cumsum(dest_hot, axis=0) - dest_hot) * dest_hot, axis=1)
    slot_index = flat_routes * capacity + slot_depth
    row_tokens = jnp.arange(2 * tok_count, dtype=jnp.int32) // 2
    send_rows = (
        jnp.zeros((req_size * capacity, model_width), jnp.bfloat16)
        .at[slot_index]
        .set(normed[row_tokens])
    )
    send_rows = send_rows.reshape(req_size, capacity, model_width)
    arrived = lax.all_to_all(send_rows, "req", split_axis=0, concat_axis=0, tiled=True)
    flat_rows = arrived.reshape(-1, model_width)
    gate_val = jnp.dot(flat_rows, gate_mat, preferred_element_type=jnp.float32)
    up_val = jnp.dot(flat_rows, up_mat, preferred_element_type=jnp.float32)
    activated = (jax.nn.silu(gate_val) * up_val).astype(jnp.bfloat16)
    partial_out = lax.dot_general(
        activated, down_mat, (((1,), (1,)), ((), ())), preferred_element_type=jnp.float32
    )
    partial_rows = partial_out.astype(jnp.bfloat16).reshape(
        arrived.shape[0], arrived.shape[1], model_width
    )
    returned_parts = lax.all_to_all(
        lax.all_to_all(partial_rows[None], "req", split_axis=1, concat_axis=1, tiled=True),
        "ffn",
        split_axis=3,
        concat_axis=0,
        tiled=True,
    )
    returned = jnp.sum(returned_parts.astype(jnp.float32), axis=0)
    expert_of = jnp.sum(dest_hot * placement[None, :], axis=1).reshape(tok_count, 2)
    expert_hot = (
        expert_of[:, :, None] == jnp.arange(EXPERTS, dtype=jnp.int32)[None, None, :]
    ).astype(jnp.float32)
    chosen = jnp.sum(router_logits[:, None, :] * expert_hot, axis=2)
    logit_peak = jnp.max(chosen, axis=1, keepdims=True)
    exp_logits = jnp.exp(chosen - logit_peak)
    gate_weights = exp_logits / jnp.sum(exp_logits, axis=1, keepdims=True)
    picked = returned.reshape(req_size * capacity, quarter)[slot_index].reshape(
        tok_count, 2, quarter
    )
    mixture = jnp.sum(picked * gate_weights[:, :, None], axis=1)
    return (own_hidden + mixture).astype(jnp.bfloat16)


def solution(mesh):
    in_specs = (
        P("req", None),
        P("req", "ffn"),
        P("req", "ffn"),
        P("req", "ffn"),
        P("req"),
        P("ffn"),
        P("ffn", "req"),
        P(),
        P("req", None),
        P("req", None),
        P(),
        P("req", None, "ffn"),
        P("req", None, "ffn"),
        P("req", None, "ffn"),
    )
    out_specs = P("req", "ffn")
    return jax.shard_map(
        per_device, mesh=mesh, in_specs=in_specs, out_specs=out_specs, check_vma=False
    )
```

profile of v0, /device:TPU:33, one launch (start us, length us, event | category | flops | bytes accessed | tf_op | source)
XLA Modules:
  0.0 685.6 jit_solution(4302674995303318617)
XLA Ops:
  25.7 211.4 %while.24 = (s32[]{:T(128)}, f32[4,2,256]{2,1,0:T(2,128)S(1)}, f32[4,2,256]{2,1,0:T(2,128)S(1)}, f32[4,2,256,128]{3,2,1,0:T(8,128)}, bf16[256,4,128]{2,0,1:T(8,1...) while((s32[]{:T(128)}, f32[4,2,256]{2,1,0:T(2,128)S(1)}, ...), condition=%wide.region_5.6_spmd.clone, body=%wide.region_2.5_spmd.clone.sunk | while | flops 551817984 | bytes 30547376 | solution.py:113
  33.0 4.5 collective-permute-start.1
  75.5 4.3 collective-permute-start
  81.8 5.9 collective-permute-done
  91.8 5.9 collective-permute-done.1
  108.2 6.1 collective-permute-done
  118.3 5.9 collective-permute-done.1
  134.7 6.1 collective-permute-done
  144.9 5.9 collective-permute-done.1
  161.3 6.1 collective-permute-done
  171.4 5.9 collective-permute-done.1
  187.8 6.1 collective-permute-done
  198.0 5.9 collective-permute-done.1
  214.4 6.1 collective-permute-done
  224.5 5.9 collective-permute-done.1
  241.7 4.7 convolution_convert_fusion.1
  248.8 74.1 %all-reduce.2.cloned.1.call-done = bf16[256,2048]{1,0:T(8,128)(2,1)} async-done(((bf16[256,2048]{1,0:T(8,128)(2,1)}), bf16[256,2048]{1,0:T(8,128)(2,1)}) %all-reduce.2.cloned.1.call-update) | async-done | bytes 1048592 | tf_op jit(solution)/shard_map/psum | solution.py:124
  327.8 11.3 %scatter_custom_fusion = bf16[640,2048]{1,0:T(8,128)(2,1)} fusion(s32[512]{0:T(512)S(1)} %bitcast.136, bf16[256,2048]{1,0:T(8,128)(2,1)} %multiply_convert_fusion, s32[1024]{0:T(1024)S(1)} %pad_clamp_fusion.1, bf16[]{:T(256)} %constant.128.clone.1), kind=kCustom, calls=%fused_computation.40 | custom fusion | bytes 2621952 | tf_op jit(solution)/shard_map/scatter | solution.py:139
  339.1 5.4 reshape.364
  344.5 107.5 %all_to_all.19 = bf16[64,10,2048]{2,1,0:T(8,128)(2,1)} all-to-all(bf16[64,10,2048]{2,1,0:T(8,128)(2,1)} %reshape.364), channel_id=1, replica_groups=mesh['req'=64,'ffn'=4] {'req'}, dimensions={0} | all-to-all | bytes 5242880 | tf_op jit(solution)/shard_map/all_to_all | solution.py:142
  452.1 5.5 reshape.365
  457.6 6.2 fusion.27
  463.8 9.7 %convolution_convert_fusion = bf16[640,2048]{1,0:T(8,128)(2,1)} fusion(bf16[1,2048,768]{2,1,0:T(8,128)(2,1)S(1)} %copy-done, f32[640,768]{1,0:T(8,128)} %fusion.27, bf16[640,2048]{1,0:T(8,128)(2,1)} %reshape.365, bf16[1,2048,768]{2,1,0:T(8,128)(2,1)} %param.28), kind=kOutput, calls=%fused_computation.32 | convolution fusion | flops 4030791680 | bytes 13500416 | tf_op jit(solution)/shard_map/dot_general | solution.py:147
  473.5 5.4 broadcast_in_dim_reshape.2
  478.8 101.9 %all_to_all.20 = bf16[1,64,10,2048]{3,2,0,1:T(8,128)(2,1)} all-to-all(bf16[1,64,10,2048]{3,2,0,1:T(8,128)(2,1)} %bitcast.121), channel_id=1, replica_groups=mesh['req'=64,'ffn'=4] {'req'}, dimensions={1} | all-to-all | bytes 5242880 | tf_op jit(solution)/shard_map/all_to_all | solution.py:154
  580.7 14.3 %copy.117 = bf16[1,64,10,2048]{1,2,0,3:T(8,128)(2,1)} copy(bf16[1,64,10,2048]{3,2,0,1:T(8,128)(2,1)} %all_to_all.20) | data formatting | bytes 5242880 | tf_op jit(solution)/shard_map/all_to_all | solution.py:154
  595.0 7.5 %reshape.404 = bf16[4,2,163840]{2,1,0:T(2,128)(2,1)} reshape(bf16[2048,1,10,64]{3,2,1,0:T(8,128)(2,1)} %bitcast.119) | data formatting | bytes 5242880
  607.0 30.6 %all-to-all-done.2 = bf16[4,2,163840]{2,1,0:T(2,128)(2,1)S(1)} async-done(((bf16[4,2,163840]{2,1,0:T(2,128)(2,1)}), bf16[4,2,163840]{2,1,0:T(2,128)(2,1)S(1)}, u32[]{:S(2)}, u32[]{:S(2)}) %all-to-all-start.2) | async-done | bytes 2621472 | tf_op jit(solution)/shard_map/all_to_all | solution.py:153
  637.7 5.8 reshape.405
  643.5 7.9 %copy.118 = bf16[1,64,10,2048]{3,1,2,0:T(8,128)(2,1)S(1)} copy(bf16[1,64,10,2048]{1,2,0,3:T(8,128)(2,1)} %bitcast.120) | data formatting | bytes 5242880 | tf_op jit(solution)/shard_map/all_to_all | solution.py:153
  651.4 5.5 reshape.368
  656.8 6.8 reduce_sum.94
  (246 shorter events, 180.3 us)
Async XLA Ops:
  6.5 235.2 %all-gather.2.cloned.1.call-start = ((), (), s32[]{:S(2)}) async-start(), calls=%async_computation.3 | async-start | bytes 4259840 | tf_op jit(solution)/shard_map/all_gather | solution.py:121
  7.3 315.6 %all-reduce.2.cloned.1.call-start = ((), (), s32[]{:S(2)}) async-start(), calls=%async_computation.4 | async-start | bytes 2097152 | tf_op jit(solution)/shard_map/psum | solution.py:124
  29.4 8.3 %collective-permute-start.2 = (bf16[256,4,128]{2,0,1:T(8,128)(2,1)}, bf16[256,4,128]{2,0,1:T(8,128)(2,1)}, u32[]{:S(2)}, u32[]{:S(2)}) collective-permute-start(bf16[256,4,128]{2,0,1:T(8,128)(2,1)} %get-tuple-element.447), channel_id=1, source_target_pairs={{0,4},{4,8},{8,12},{12,16},{16,20},{20,24},{24,28},{28,32},{32,36}... | collective-permute-start | bytes 786440 | tf_op jit(solution)/shard_map/while/body/eval_jaxpr/ppermute | solution.py:18
  33.0 8.2 %collective-permute-start.1 = (bf16[256,4,128]{2,0,1:T(8,128)(2,1)}, bf16[256,4,128]{2,0,1:T(8,128)(2,1)S(1)}, u32[]{:S(2)}, u32[]{:S(2)}) collective-permute-start(bf16[256,4,128]{2,0,1:T(8,128)(2,1)} %collective-permute-done), channel_id=1, source_target_pairs={{0,4},{4,8},{8,12},{12,16},{16,20},{20,24},{24,28},{28,32},{32,36}... | collective-permute-start | bytes 786440 | tf_op jit(solution)/shard_map/while/body/eval_jaxpr/ppermute | solution.py:18
  47.9 9.1 %collective-permute-start = (bf16[256,4,128]{2,0,1:T(8,128)(2,1)S(1)}, bf16[256,4,128]{2,0,1:T(8,128)(2,1)}, u32[]{:S(2)}, u32[]{:S(2)}) collective-permute-start(bf16[256,4,128]{2,0,1:T(8,128)(2,1)S(1)} %get-tuple-element.446), channel_id=1, source_target_pairs={{0,4},{4,8},{8,12},{12,16},{16,20},{20,24},{24,28},{28,32},{32,36}... | collective-permute-start | bytes 786440 | tf_op jit(solution)/shard_map/while/body/eval_jaxpr/ppermute | solution.py:18
  57.0 10.0 %collective-permute-start.1 = (bf16[256,4,128]{2,0,1:T(8,128)(2,1)}, bf16[256,4,128]{2,0,1:T(8,128)(2,1)S(1)}, u32[]{:S(2)}, u32[]{:S(2)}) collective-permute-start(bf16[256,4,128]{2,0,1:T(8,128)(2,1)} %collective-permute-done), channel_id=1, source_target_pairs={{0,4},{4,8},{8,12},{12,16},{16,20},{20,24},{24,28},{28,32},{32,36}... | collective-permute-start | bytes 786440 | tf_op jit(solution)/shard_map/while/body/eval_jaxpr/ppermute | solution.py:18
  60.2 11.7 %collective-permute-start.3 = (bf16[256,4,128]{2,0,1:T(8,128)(2,1)}, bf16[256,4,128]{2,0,1:T(8,128)(2,1)S(1)}, u32[]{:S(2)}, u32[]{:S(2)}) collective-permute-start(bf16[256,4,128]{2,0,1:T(8,128)(2,1)} %collective-permute-done.2), channel_id=1, source_target_pairs={{0,4},{4,8},{8,12},{12,16},{16,20},{20,24},{24,28},{28,32},{32,36}... | collective-permute-start | bytes 786440 | tf_op jit(solution)/shard_map/while/body/eval_jaxpr/ppermute | solution.py:18
  75.5 12.2 %collective-permute-start = (bf16[256,4,128]{2,0,1:T(8,128)(2,1)S(1)}, bf16[256,4,128]{2,0,1:T(8,128)(2,1)}, u32[]{:S(2)}, u32[]{:S(2)}) collective-permute-start(bf16[256,4,128]{2,0,1:T(8,128)(2,1)S(1)} %get-tuple-element.446), channel_id=1, source_target_pairs={{0,4},{4,8},{8,12},{12,16},{16,20},{20,24},{24,28},{28,32},{32,36}... | collective-permute-start | bytes 786440 | tf_op jit(solution)/shard_map/while/body/eval_jaxpr/ppermute | solution.py:18
  79.8 10.0 %collective-permute-start.2 = (bf16[256,4,128]{2,0,1:T(8,128)(2,1)}, bf16[256,4,128]{2,0,1:T(8,128)(2,1)}, u32[]{:S(2)}, u32[]{:S(2)}) collective-permute-start(bf16[256,4,128]{2,0,1:T(8,128)(2,1)} %get-tuple-element.447), channel_id=1, source_target_pairs={{0,4},{4,8},{8,12},{12,16},{16,20},{20,24},{24,28},{28,32},{32,36}... | collective-permute-start | bytes 786440 | tf_op jit(solution)/shard_map/while/body/eval_jaxpr/ppermute | solution.py:18
  87.7 10.0 %collective-permute-start.1 = (bf16[256,4,128]{2,0,1:T(8,128)(2,1)}, bf16[256,4,128]{2,0,1:T(8,128)(2,1)S(1)}, u32[]{:S(2)}, u32[]{:S(2)}) collective-permute-start(bf16[256,4,128]{2,0,1:T(8,128)(2,1)} %collective-permute-done), channel_id=1, source_target_pairs={{0,4},{4,8},{8,12},{12,16},{16,20},{20,24},{24,28},{28,32},{32,36}... | collective-permute-start | bytes 786440 | tf_op jit(solution)/shard_map/while/body/eval_jaxpr/ppermute | solution.py:18
  89.9 10.6 %collective-permute-start.3 = (bf16[256,4,128]{2,0,1:T(8,128)(2,1)}, bf16[256,4,128]{2,0,1:T(8,128)(2,1)S(1)}, u32[]{:S(2)}, u32[]{:S(2)}) collective-permute-start(bf16[256,4,128]{2,0,1:T(8,128)(2,1)} %collective-permute-done.2), channel_id=1, source_target_pairs={{0,4},{4,8},{8,12},{12,16},{16,20},{20,24},{24,28},{28,32},{32,36}... | collective-permute-start | bytes 786440 | tf_op jit(solution)/shard_map/while/body/eval_jaxpr/ppermute | solution.py:18
  104.3 9.9 %collective-permute-start = (bf16[256,4,128]{2,0,1:T(8,128)(2,1)S(1)}, bf16[256,4,128]{2,0,1:T(8,128)(2,1)}, u32[]{:S(2)}, u32[]{:S(2)}) collective-permute-start(bf16[256,4,128]{2,0,1:T(8,128)(2,1)S(1)} %get-tuple-element.446), channel_id=1, source_target_pairs={{0,4},{4,8},{8,12},{12,16},{16,20},{20,24},{24,28},{28,32},{32,36}... | collective-permute-start | bytes 786440 | tf_op jit(solution)/shard_map/while/body/eval_jaxpr/ppermute | solution.py:18
  106.2 10.2 %collective-permute-start.2 = (bf16[256,4,128]{2,0,1:T(8,128)(2,1)}, bf16[256,4,128]{2,0,1:T(8,128)(2,1)}, u32[]{:S(2)}, u32[]{:S(2)}) collective-permute-start(bf16[256,4,128]{2,0,1:T(8,128)(2,1)} %get-tuple-element.447), channel_id=1, source_target_pairs={{0,4},{4,8},{8,12},{12,16},{16,20},{20,24},{24,28},{28,32},{32,36}... | collective-permute-start | bytes 786440 | tf_op jit(solution)/shard_map/while/body/eval_jaxpr/ppermute | solution.py:18
  114.2 10.0 %collective-permute-start.1 = (bf16[256,4,128]{2,0,1:T(8,128)(2,1)}, bf16[256,4,128]{2,0,1:T(8,128)(2,1)S(1)}, u32[]{:S(2)}, u32[]{:S(2)}) collective-permute-start(bf16[256,4,128]{2,0,1:T(8,128)(2,1)} %collective-permute-done), channel_id=1, source_target_pairs={{0,4},{4,8},{8,12},{12,16},{16,20},{20,24},{24,28},{28,32},{32,36}... | collective-permute-start | bytes 786440 | tf_op jit(solution)/shard_map/while/body/eval_jaxpr/ppermute | solution.py:18
  116.4 10.6 %collective-permute-start.3 = (bf16[256,4,128]{2,0,1:T(8,128)(2,1)}, bf16[256,4,128]{2,0,1:T(8,128)(2,1)S(1)}, u32[]{:S(2)}, u32[]{:S(2)}) collective-permute-start(bf16[256,4,128]{2,0,1:T(8,128)(2,1)} %collective-permute-done.2), channel_id=1, source_target_pairs={{0,4},{4,8},{8,12},{12,16},{16,20},{20,24},{24,28},{28,32},{32,36}... | collective-permute-start | bytes 786440 | tf_op jit(solution)/shard_map/while/body/eval_jaxpr/ppermute | solution.py:18
  130.9 9.9 %collective-permute-start = (bf16[256,4,128]{2,0,1:T(8,128)(2,1)S(1)}, bf16[256,4,128]{2,0,1:T(8,128)(2,1)}, u32[]{:S(2)}, u32[]{:S(2)}) collective-permute-start(bf16[256,4,128]{2,0,1:T(8,128)(2,1)S(1)} %get-tuple-element.446), channel_id=1, source_target_pairs={{0,4},{4,8},{8,12},{12,16},{16,20},{20,24},{24,28},{28,32},{32,36}... | collective-permute-start | bytes 786440 | tf_op jit(solution)/shard_map/while/body/eval_jaxpr/ppermute | solution.py:18
  132.8 10.2 %collective-permute-start.2 = (bf16[256,4,128]{2,0,1:T(8,128)(2,1)}, bf16[256,4,128]{2,0,1:T(8,128)(2,1)}, u32[]{:S(2)}, u32[]{:S(2)}) collective-permute-start(bf16[256,4,128]{2,0,1:T(8,128)(2,1)} %get-tuple-element.447), channel_id=1, source_target_pairs={{0,4},{4,8},{8,12},{12,16},{16,20},{20,24},{24,28},{28,32},{32,36}... | collective-permute-start | bytes 786440 | tf_op jit(solution)/shard_map/while/body/eval_jaxpr/ppermute | solution.py:18
  140.8 10.0 %collective-permute-start.1 = (bf16[256,4,128]{2,0,1:T(8,128)(2,1)}, bf16[256,4,128]{2,0,1:T(8,128)(2,1)S(1)}, u32[]{:S(2)}, u32[]{:S(2)}) collective-permute-start(bf16[256,4,128]{2,0,1:T(8,128)(2,1)} %collective-permute-done), channel_id=1, source_target_pairs={{0,4},{4,8},{8,12},{12,16},{16,20},{20,24},{24,28},{28,32},{32,36}... | collective-permute-start | bytes 786440 | tf_op jit(solution)/shard_map/while/body/eval_jaxpr/ppermute | solution.py:18
  143.0 10.6 %collective-permute-start.3 = (bf16[256,4,128]{2,0,1:T(8,128)(2,1)}, bf16[256,4,128]{2,0,1:T(8,128)(2,1)S(1)}, u32[]{:S(2)}, u32[]{:S(2)}) collective-permute-start(bf16[256,4,128]{2,0,1:T(8,128)(2,1)} %collective-permute-done.2), channel_id=1, source_target_pairs={{0,4},{4,8},{8,12},{12,16},{16,20},{20,24},{24,28},{28,32},{32,36}... | collective-permute-start | bytes 786440 | tf_op jit(solution)/shard_map/while/body/eval_jaxpr/ppermute | solution.py:18
  157.4 9.9 %collective-permute-start = (bf16[256,4,128]{2,0,1:T(8,128)(2,1)S(1)}, bf16[256,4,128]{2,0,1:T(8,128)(2,1)}, u32[]{:S(2)}, u32[]{:S(2)}) collective-permute-start(bf16[256,4,128]{2,0,1:T(8,128)(2,1)S(1)} %get-tuple-element.446), channel_id=1, source_target_pairs={{0,4},{4,8},{8,12},{12,16},{16,20},{20,24},{24,28},{28,32},{32,36}... | collective-permute-start | bytes 786440 | tf_op jit(solution)/shard_map/while/body/eval_jaxpr/ppermute | solution.py:18
  159.3 10.2 %collective-permute-start.2 = (bf16[256,4,128]{2,0,1:T(8,128)(2,1)}, bf16[256,4,128]{2,0,1:T(8,128)(2,1)}, u32[]{:S(2)}, u32[]{:S(2)}) collective-permute-start(bf16[256,4,128]{2,0,1:T(8,128)(2,1)} %get-tuple-element.447), channel_id=1, source_target_pairs={{0,4},{4,8},{8,12},{12,16},{16,20},{20,24},{24,28},{28,32},{32,36}... | collective-permute-start | bytes 786440 | tf_op jit(solution)/shard_map/while/body/eval_jaxpr/ppermute | solution.py:18
  167.3 10.0 %collective-permute-start.1 = (bf16[256,4,128]{2,0,1:T(8,128)(2,1)}, bf16[256,4,128]{2,0,1:T(8,128)(2,1)S(1)}, u32[]{:S(2)}, u32[]{:S(2)}) collective-permute-start(bf16[256,4,128]{2,0,1:T(8,128)(2,1)} %collective-permute-done), channel_id=1, source_target_pairs={{0,4},{4,8},{8,12},{12,16},{16,20},{20,24},{24,28},{28,32},{32,36}... | collective-permute-start | bytes 786440 | tf_op jit(solution)/shard_map/while/body/eval_jaxpr/ppermute | solution.py:18
  169.5 10.6 %collective-permute-start.3 = (bf16[256,4,128]{2,0,1:T(8,128)(2,1)}, bf16[256,4,128]{2,0,1:T(8,128)(2,1)S(1)}, u32[]{:S(2)}, u32[]{:S(2)}) collective-permute-start(bf16[256,4,128]{2,0,1:T(8,128)(2,1)} %collective-permute-done.2), channel_id=1, source_target_pairs={{0,4},{4,8},{8,12},{12,16},{16,20},{20,24},{24,28},{28,32},{32,36}... | collective-permute-start | bytes 786440 | tf_op jit(solution)/shard_map/while/body/eval_jaxpr/ppermute | solution.py:18
  184.0 9.9 %collective-permute-start = (bf16[256,4,128]{2,0,1:T(8,128)(2,1)S(1)}, bf16[256,4,128]{2,0,1:T(8,128)(2,1)}, u32[]{:S(2)}, u32[]{:S(2)}) collective-permute-start(bf16[256,4,128]{2,0,1:T(8,128)(2,1)S(1)} %get-tuple-element.446), channel_id=1, source_target_pairs={{0,4},{4,8},{8,12},{12,16},{16,20},{20,24},{24,28},{28,32},{32,36}... | collective-permute-start | bytes 786440 | tf_op jit(solution)/shard_map/while/body/eval_jaxpr/ppermute | solution.py:18
  185.9 10.2 %collective-permute-start.2 = (bf16[256,4,128]{2,0,1:T(8,128)(2,1)}, bf16[256,4,128]{2,0,1:T(8,128)(2,1)}, u32[]{:S(2)}, u32[]{:S(2)}) collective-permute-start(bf16[256,4,128]{2,0,1:T(8,128)(2,1)} %get-tuple-element.447), channel_id=1, source_target_pairs={{0,4},{4,8},{8,12},{12,16},{16,20},{20,24},{24,28},{28,32},{32,36}... | collective-permute-start | bytes 786440 | tf_op jit(solution)/shard_map/while/body/eval_jaxpr/ppermute | solution.py:18
  193.9 10.0 %collective-permute-start.1 = (bf16[256,4,128]{2,0,1:T(8,128)(2,1)}, bf16[256,4,128]{2,0,1:T(8,128)(2,1)S(1)}, u32[]{:S(2)}, u32[]{:S(2)}) collective-permute-start(bf16[256,4,128]{2,0,1:T(8,128)(2,1)} %collective-permute-done), channel_id=1, source_target_pairs={{0,4},{4,8},{8,12},{12,16},{16,20},{20,24},{24,28},{28,32},{32,36}... | collective-permute-start | bytes 786440 | tf_op jit(solution)/shard_map/while/body/eval_jaxpr/ppermute | solution.py:18
  196.0 10.6 %collective-permute-start.3 = (bf16[256,4,128]{2,0,1:T(8,128)(2,1)}, bf16[256,4,128]{2,0,1:T(8,128)(2,1)S(1)}, u32[]{:S(2)}, u32[]{:S(2)}) collective-permute-start(bf16[256,4,128]{2,0,1:T(8,128)(2,1)} %collective-permute-done.2), channel_id=1, source_target_pairs={{0,4},{4,8},{8,12},{12,16},{16,20},{20,24},{24,28},{28,32},{32,36}... | collective-permute-start | bytes 786440 | tf_op jit(solution)/shard_map/while/body/eval_jaxpr/ppermute | solution.py:18
  210.5 9.9 %collective-permute-start = (bf16[256,4,128]{2,0,1:T(8,128)(2,1)S(1)}, bf16[256,4,128]{2,0,1:T(8,128)(2,1)}, u32[]{:S(2)}, u32[]{:S(2)}) collective-permute-start(bf16[256,4,128]{2,0,1:T(8,128)(2,1)S(1)} %get-tuple-element.446), channel_id=1, source_target_pairs={{0,4},{4,8},{8,12},{12,16},{16,20},{20,24},{24,28},{28,32},{32,36}... | collective-permute-start | bytes 786440 | tf_op jit(solution)/shard_map/while/body/eval_jaxpr/ppermute | solution.py:18
  212.4 10.2 %collective-permute-start.2 = (bf16[256,4,128]{2,0,1:T(8,128)(2,1)}, bf16[256,4,128]{2,0,1:T(8,128)(2,1)}, u32[]{:S(2)}, u32[]{:S(2)}) collective-permute-start(bf16[256,4,128]{2,0,1:T(8,128)(2,1)} %get-tuple-element.447), channel_id=1, source_target_pairs={{0,4},{4,8},{8,12},{12,16},{16,20},{20,24},{24,28},{28,32},{32,36}... | collective-permute-start | bytes 786440 | tf_op jit(solution)/shard_map/while/body/eval_jaxpr/ppermute | solution.py:18
  220.4 10.0 %collective-permute-start.1 = (bf16[256,4,128]{2,0,1:T(8,128)(2,1)}, bf16[256,4,128]{2,0,1:T(8,128)(2,1)S(1)}, u32[]{:S(2)}, u32[]{:S(2)}) collective-permute-start(bf16[256,4,128]{2,0,1:T(8,128)(2,1)} %collective-permute-done), channel_id=1, source_target_pairs={{0,4},{4,8},{8,12},{12,16},{16,20},{20,24},{24,28},{28,32},{32,36}... | collective-permute-start | bytes 786440 | tf_op jit(solution)/shard_map/while/body/eval_jaxpr/ppermute | solution.py:18
  222.6 10.6 %collective-permute-start.3 = (bf16[256,4,128]{2,0,1:T(8,128)(2,1)}, bf16[256,4,128]{2,0,1:T(8,128)(2,1)S(1)}, u32[]{:S(2)}, u32[]{:S(2)}) collective-permute-start(bf16[256,4,128]{2,0,1:T(8,128)(2,1)} %collective-permute-done.2), channel_id=1, source_target_pairs={{0,4},{4,8},{8,12},{12,16},{16,20},{20,24},{24,28},{28,32},{32,36}... | collective-permute-start | bytes 786440 | tf_op jit(solution)/shard_map/while/body/eval_jaxpr/ppermute | solution.py:18
  602.6 35.1 %all-to-all-start.2 = ((bf16[4,2,163840]{2,1,0:T(2,128)(2,1)}), bf16[4,2,163840]{2,1,0:T(2,128)(2,1)S(1)}, u32[]{:S(2)}, u32[]{:S(2)}) async-start(bf16[4,2,163840]{2,1,0:T(2,128)(2,1)} %reshape.404), calls=%async_computation.2 | async-start | bytes 5242880 | tf_op jit(solution)/shard_map/all_to_all | solution.py:153
  (38 other events, 651.4 us)
Sparse Core Ops, SparseCore 0:
  10.1 83.5 all-gather.1
  246.5 76.3 all-reduce.1
where the time goes:
time: 696 us; the launch traced here: 686 us
  blocking collectives  209 us (30%)
  waiting for transfers between devices  189 us (27%)
  local copies, waits for them, and re-layouts  105 us (15%)
  starting transfers between devices  76.7 us (11%)
  matrix products  60.6 us (9%)
  other arithmetic  29.8 us (4%)
  between operations  13.9 us (2%)
    all_to_all x1, blocking collectives, per_device(): lax.all_to_all(send_rows, 'req', split_axis=0, concat_axis=0, tiled=True)  108 us
    all_to_all x1, blocking collectives, per_device(): lax.all_to_all(partial_rows[None], 'req', split_axis=1, concat_axis=1, ti...  102 us
    ppermute x32, waiting for transfers between devices, shifted(): lax.ppermute(value, axis, [(source, source + steps) for source in range(i...  83.3 us
    psum x1, waiting for transfers between devices, per_device(): summed = lax.psum(proj.astype(jnp.bfloat16), 'ffn').astype(jnp.float32)  74.1 us
    ppermute x32, starting transfers between devices, shifted(): lax.ppermute(value, axis, [(source, source + steps) for source in range(i...  72.7 us
    all_to_all x1, waiting for transfers between devices, per_device(): lax.all_to_all(lax.all_to_all(partial_rows[None], 'req', split_axis=1, co...  30.6 us
    unnamed x31, local copies, waits for them, and re-layouts  25.2 us
    dot_general x9, matrix products, attend(): jnp.einsum('plyw,wpj->plyj', probs.astype(jnp.bfloat16), values_in_block,...  23.6 us
  transfers between devices with their start and end apart: 35, of which 19 were waited for; matrix products, arithmetic and copies ran while one was open for 10% of the time, Pallas kernels for 0%

commit v1 on v0

v1 whole, which is shorter than its diff:
```python
import jax
import jax.numpy as jnp
from jax import lax
from jax.experimental import pallas as pl
from jax.experimental.pallas import tpu as pltpu
from jax.sharding import PartitionSpec as P

QUERY_HEADS = 32
KEY_VALUE_HEADS = 16
HEAD_SIZE = 128
EXPERTS = 8
EPS = 1e-06
MESH = pl.DeviceIdType.MESH
BF = jnp.bfloat16
F32 = jnp.float32

NREQ = 64
NFFN = 4
NZ = 8
TOK = 256
D = 2048
Q = D // NFFN
HID = 768
WIDE = Q + 128
Z_ORDER = (0, 1, 7, 2, 6, 3, 5, 4)


def dot(a, b):
    return jnp.dot(a, b, preferred_element_type=F32)


def dot_nt(a, b):
    return lax.dot_general(a, b, (((1,), (1,)), ((), ())), preferred_element_type=F32)


def iota(shape, dim):
    return lax.broadcasted_iota(jnp.int32, shape, dim)


def remote(src, dst, send_sem, recv_sem, req, ffn):
    return pltpu.make_async_remote_copy(
        src_ref=src, dst_ref=dst, send_sem=send_sem, recv_sem=recv_sem,
        device_id=(req, ffn), device_id_type=MESH,
    )


def layer_kernel(
    att_ref, wo_hbm, res_hbm, gain_hbm, logits_ref, routes_ref, placement_ref, wg_hbm, wu_hbm, wd_hbm,
    out_ref,
    wo, res, gain, wg, wu, wd,
    proj_send, proj_recv, hid, stat_send, stat_recv,
    e_main, e_rem, g_main, g_rem,
    disp, rows, xbuf, act, part, hop_l, hop_r, from_l, from_r, fin, ret,
    in_sem, proj_ssem, proj_rsem, stat_ssem, stat_rsem,
    a2a_ssem, a2a_rsem, ag_ssem, ag_rsem, rs_ssem, rs_rsem, ret_ssem, ret_rsem, own_sem,
):
    r = lax.axis_index("req")
    y = lax.axis_index("ffn")
    z = r // 8
    yp, ym, y2 = lax.rem(y + 1, 4), lax.rem(y + 3, 4), lax.rem(y + 2, 4)
    peers = (yp, y2, ym)

    bar = pltpu.get_barrier_semaphore()

    def greet(o, c):
        pl.semaphore_signal(bar, inc=1, device_id=(lax.rem(r + o, NREQ), y), device_id_type=MESH)
        return c

    lax.fori_loop(1, NREQ, greet, 0)
    for p in peers:
        pl.semaphore_signal(bar, inc=1, device_id=(r, p), device_id_type=MESH)

    y_cols = pl.ds(pl.multiple_of(y * Q, Q), Q)
    loads = [
        pltpu.make_async_copy(wo_hbm, wo, in_sem.at[0]),
        pltpu.make_async_copy(res_hbm.at[:, y_cols], res, in_sem.at[1]),
        pltpu.make_async_copy(gain_hbm.at[:, y_cols], gain, in_sem.at[2]),
        pltpu.make_async_copy(wg_hbm, wg, in_sem.at[3]),
        pltpu.make_async_copy(wu_hbm, wu, in_sem.at[4]),
        pltpu.make_async_copy(wd_hbm, wd, in_sem.at[5]),
    ]
    for load in loads:
        load.start()

    route0, route1 = routes_ref[0:1, :], routes_ref[1:2, :]
    dest = iota((NREQ, TOK), 0)
    hot0 = jnp.where(dest == route0, 1.0, 0.0)
    hot1 = jnp.where(dest == route1, 1.0, 0.0)
    before = jnp.where(iota((TOK, TOK), 0) < iota((TOK, TOK), 1), 1.0, 0.0).astype(BF)
    earlier = dot((hot0 + hot1).astype(BF), before)
    slot0 = route0.astype(F32) * 16.0 + jnp.sum(hot0 * earlier, axis=0, keepdims=True)
    slot1 = route1.astype(F32) * 16.0 + jnp.sum(hot1 * (earlier + hot0), axis=0, keepdims=True)
    line = iota((512, TOK), 0)
    main_id = ((line >> 3) * 16 + (line & 7)).astype(F32)
    rem_id = ((line >> 3) * 16 + 8 + (line & 1)).astype(F32)
    e_main[...] = jnp.where((main_id == slot0) | (main_id == slot1), 1.0, 0.0).astype(BF)
    e_rem[...] = jnp.where((rem_id == slot0) | (rem_id == slot1), 1.0, 0.0).astype(BF)
    hosts = jnp.where(iota((EXPERTS, NREQ), 0) == placement_ref[...], 1.0, 0.0).astype(BF)
    logits = logits_ref[...]
    pick0 = jnp.sum(logits * dot(hosts, hot0.astype(BF)), axis=0, keepdims=True)
    pick1 = jnp.sum(logits * dot(hosts, hot1.astype(BF)), axis=0, keepdims=True)
    top = jnp.maximum(pick0, pick1)
    exp0, exp1 = jnp.exp(pick0 - top), jnp.exp(pick1 - top)
    total = exp0 + exp1
    sub = iota((128, TOK), 0)
    packed = jnp.where(sub == 0, slot0, jnp.where(sub == 1, slot1, jnp.where(sub == 2, exp0 / total, exp1 / total)))
    turned = packed.T
    s0, s1, w0, w1 = turned[:, 0:1], turned[:, 1:2], turned[:, 2:3], turned[:, 3:4]
    col = iota((TOK, 512), 1)
    for ids, ref in (((col >> 3) * 16 + (col & 7), g_main), ((col >> 3) * 16 + 8 + (col & 1), g_rem)):
        ids = ids.astype(F32)
        gate = jnp.where(ids == s0, w0, 0.0) + jnp.where(ids == s1, w1, 0.0)
        high = gate.astype(BF)
        ref[0] = high
        ref[1] = (gate - high.astype(F32)).astype(BF)

    pl.semaphore_wait(bar, NREQ - 1 + 3)

    loads[0].wait()

    def project(which):
        return dot_nt(att_ref[...], wo[pl.ds(pl.multiple_of(which * Q, Q), Q), :])

    proj_copies = []
    for i in (1, 0, 2):
        proj_send[i] = project(peers[i]).astype(BF)
        copy = remote(proj_send.at[i], proj_recv.at[2 - i], proj_ssem.at[i], proj_rsem.at[2 - i], r, peers[i])
        copy.start()
        proj_copies.append(copy)
    loads[1].wait()
    own = res[...].astype(F32) + project(y)
    for i in range(3):
        pltpu.make_async_copy(proj_recv.at[i], proj_recv.at[i], proj_rsem.at[i]).wait()
    hidden = own + proj_recv[0].astype(F32) + proj_recv[1].astype(F32) + proj_recv[2].astype(F32)
    hid[...] = hidden

    square = jnp.sum(hidden * hidden, axis=1, keepdims=True)
    stat_send[...] = jnp.broadcast_to(square, (TOK, 128)).T[0:8, :]
    stat_copies = []
    for i in range(3):
        copy = remote(stat_send, stat_recv.at[2 - i], stat_ssem.at[i], stat_rsem.at[2 - i], r, peers[i])
        copy.start()
        stat_copies.append(copy)
    loads[2].wait()
    for i in range(3):
        pltpu.make_async_copy(stat_recv.at[i], stat_recv.at[i], stat_rsem.at[i]).wait()
    squares = stat_send[...] + stat_recv[0] + stat_recv[1] + stat_recv[2]
    factor = lax.rsqrt(squares[0:1, :] * (1.0 / D) + EPS)
    factor = jnp.broadcast_to(factor, (128, TOK)).T[:, 0:1]
    normed = (hidden * factor * gain[...]).astype(BF)

    disp2 = disp.reshape(512, WIDE)
    disp2[:, 0:Q] = dot(e_main[...], normed).astype(BF)
    spread = dot(e_rem[...], normed)
    piece = (iota((512, 128), 0) & 7) >> 1

    def by_piece(parts):
        return jnp.where(piece == 0, parts[0], jnp.where(piece == 1, parts[1], jnp.where(piece == 2, parts[2], parts[3])))

    disp2[:, Q:WIDE] = by_piece([spread[:, 128 * k:128 * k + 128] for k in range(4)]).astype(BF)

    def exchange(source, target, send_sem, recv_sems):
        for dz in Z_ORDER:
            def push(k, c):
                d = lax.rem(z + dz, NZ) * 8 + lax.rem(r + k, 8)
                remote(source.at[d], target.at[r], send_sem, recv_sems.at[z], d, y).start()
                return c
            lax.fori_loop(1 if dz == 0 else 0, 8, push, 0)
        copy = pltpu.make_async_copy(source.at[r], target.at[r], own_sem)
        copy.start()
        copy.wait()

    def arrived(target, recv_sems, dz):
        g = lax.rem(z + dz, NZ)
        count = 7 if dz == 0 else 8
        view = target.at[pl.ds(g * 8, count)]
        pltpu.make_async_copy(view, view, recv_sems.at[g]).wait()

    mine = rows.at[y]
    exchange(disp, mine, a2a_ssem, a2a_rsem)

    ag_copies = []

    def forward(i):
        g = pl.ds(lax.rem(z + Z_ORDER[i], NZ) * 8, 8)
        here, there, side = (ym, yp, 0) if i % 2 == 0 else (yp, ym, 1)
        view = rows.at[here, g]
        pltpu.make_async_copy(view, view, ag_rsem.at[side, i]).wait()
        copy = remote(view, view, ag_ssem.at[2, i], ag_rsem.at[2, i], r, there)
        copy.start()
        ag_copies.append(copy)

    for i, dz in enumerate(Z_ORDER):
        arrived(mine, a2a_rsem, dz)
        g = pl.ds(lax.rem(z + dz, NZ) * 8, 8)
        view = rows.at[y, g]
        for side, there in ((0, yp), (1, ym)):
            copy = remote(view, view, ag_ssem.at[side, i], ag_rsem.at[side, i], r, there)
            copy.start()
            ag_copies.append(copy)
        if i > 0:
            forward(i - 1)
    forward(7)
    for i in range(8):
        g = pl.ds(lax.rem(z + Z_ORDER[i], NZ) * 8, 8)
        here, side = (yp, 1) if i % 2 == 0 else (ym, 0)
        view = rows.at[here, g]
        pltpu.make_async_copy(view, view, ag_rsem.at[side, i]).wait()
        view = rows.at[y2, g]
        pltpu.make_async_copy(view, view, ag_rsem.at[2, i]).wait()

    rows2 = rows.reshape(4, 512, WIDE)
    row_id = iota((128, 512), 0)
    line_id = iota((128, 512), 1)
    for q in range(4):
        xbuf[0:512, Q * q:Q * q + Q] = rows2[q, :, 0:Q]
    for k in range(4):
        select = jnp.where(line_id == (row_id >> 1) * 8 + 2 * k + (row_id & 1), 1.0, 0.0).astype(BF)
        for q in range(4):
            xbuf[512:640, Q * q + 128 * k:Q * q + 128 * k + 128] = dot(select, rows2[q, :, Q:WIDE]).astype(BF)
    loads[3].wait()
    loads[4].wait()

    def inner(n, c):
        cols = pl.ds(pl.multiple_of(n * 256, 256), 256)
        gate = dot(xbuf[...], wg[:, cols])
        up = dot(xbuf[...], wu[:, cols])
        act[:, cols] = (gate / (1.0 + jnp.exp(-gate)) * up).astype(BF)
        return c

    lax.fori_loop(0, HID // 256, inner, 0)
    loads[5].wait()

    line_of = iota((512, 512), 0)
    row_of = iota((512, 512), 1)
    scatter = jnp.where(
        line_of == ((row_of & 127) >> 1) * 8 + 2 * (row_of >> 7) + (row_of & 1), 1.0, 0.0
    ).astype(BF)
    part2 = part.reshape(4, 512, WIDE)
    for j, which in enumerate((y2, yp, ym, y)):
        piece_out = dot_nt(act[...], wd[pl.ds(pl.multiple_of(which * Q, Q), Q), :])
        part2[j, :, 0:Q] = piece_out[0:512].astype(BF)
        tail = piece_out[512:640].astype(BF)
        stacked = jnp.concatenate([tail[:, 128 * k:128 * k + 128] for k in range(4)], axis=0)
        part2[j, :, Q:WIDE] = dot(scatter, stacked).astype(BF)
        if j == 0:
            rs = [
                remote(part.at[0, pl.ds(0, 32)], hop_l, rs_ssem.at[0], rs_rsem.at[0], r, yp),
                remote(part.at[0, pl.ds(32, 32)], hop_r, rs_ssem.at[1], rs_rsem.at[1], r, ym),
            ]
            rs[0].start()
            rs[1].start()
        if j == 1:
            rs.append(remote(part.at[1, pl.ds(32, 32)], from_l.at[pl.ds(32, 32)], rs_ssem.at[2], rs_rsem.at[2], r, yp))
            rs[2].start()
        if j == 2:
            rs.append(remote(part.at[2, pl.ds(0, 32)], from_r.at[pl.ds(0, 32)], rs_ssem.at[3], rs_rsem.at[3], r, ym))
            rs[3].start()
    hop_l2, hop_r2 = hop_l.reshape(256, WIDE), hop_r.reshape(256, WIDE)
    pltpu.make_async_copy(hop_l, hop_l, rs_rsem.at[0]).wait()
    part2[1, 0:256, :] = (part2[1, 0:256, :].astype(F32) + hop_l2[...].astype(F32)).astype(BF)
    rs.append(remote(part.at[1, pl.ds(0, 32)], from_l.at[pl.ds(0, 32)], rs_ssem.at[4], rs_rsem.at[4], r, yp))
    rs[4].start()
    pltpu.make_async_copy(hop_r, hop_r, rs_rsem.at[1]).wait()
    part2[2, 256:512, :] = (part2[2, 256:512, :].astype(F32) + hop_r2[...].astype(F32)).astype(BF)
    rs.append(remote(part.at[2, pl.ds(32, 32)], from_r.at[pl.ds(32, 32)], rs_ssem.at[5], rs_rsem.at[5], r, ym))
    rs[5].start()
    low, high = pl.ds(0, 32), pl.ds(32, 32)
    for ref, half, k in ((from_l, high, 2), (from_r, low, 3), (from_l, low, 4), (from_r, high, 5)):
        view = ref.at[half]
        pltpu.make_async_copy(view, view, rs_rsem.at[k]).wait()
    fin2 = fin.reshape(512, WIDE)
    from_l2, from_r2 = from_l.reshape(512, WIDE), from_r.reshape(512, WIDE)
    fin2[...] = (part2[3].astype(F32) + from_l2[...].astype(F32) + from_r2[...].astype(F32)).astype(BF)

    exchange(fin, ret, ret_ssem, ret_rsem)
    for dz in Z_ORDER:
        arrived(ret, ret_rsem, dz)
    ret2 = ret.reshape(512, WIDE)
    back = ret2[:, 0:Q]
    lines = ret2[:, Q:WIDE]
    masked = jnp.concatenate([jnp.where(piece == k, lines.astype(F32), 0.0).astype(BF) for k in range(4)], axis=1)
    mixture = dot(g_main[0], back) + dot(g_main[1], back) + dot(g_rem[0], masked) + dot(g_rem[1], masked)
    out_ref[...] = (hid[...] + mixture).astype(BF)

    for copy in proj_copies + stat_copies + ag_copies + rs:
        copy.wait_send()
    for sem, ref in ((a2a_ssem, disp), (ret_ssem, fin)):
        view = ref.at[pl.ds(0, NREQ - 1)]
        pltpu.make_async_copy(view, view, sem).wait()


def layer_call(att, wo, residual, gain, logits, routes, placement, wg, wu, wd):
    vmem = pl.BlockSpec(memory_space=pltpu.VMEM)
    hbm = pl.BlockSpec(memory_space=pl.ANY)
    dma = pltpu.SemaphoreType.DMA
    chunk = (NREQ, 8, WIDE)
    return pl.pallas_call(
        layer_kernel,
        out_shape=jax.ShapeDtypeStruct((TOK, Q), BF),
        in_specs=[vmem, hbm, hbm, hbm, vmem, vmem, vmem, hbm, hbm, hbm],
        out_specs=vmem,
        scratch_shapes=[
            pltpu.VMEM((D, D // 2), BF), pltpu.VMEM((TOK, Q), BF), pltpu.VMEM((1, Q), F32),
            pltpu.VMEM((D, HID), BF), pltpu.VMEM((D, HID), BF), pltpu.VMEM((D, HID), BF),
            pltpu.VMEM((3, TOK, Q), BF), pltpu.VMEM((3, TOK, Q), BF), pltpu.VMEM((TOK, Q), F32),
            pltpu.VMEM((8, TOK), F32), pltpu.VMEM((3, 8, TOK), F32),
            pltpu.VMEM((512, TOK), BF), pltpu.VMEM((512, TOK), BF),
            pltpu.VMEM((2, TOK, 512), BF), pltpu.VMEM((2, TOK, 512), BF),
            pltpu.VMEM(chunk, BF), pltpu.VMEM((4,) + chunk, BF), pltpu.VMEM((640, D), BF), pltpu.VMEM((640, HID), BF),
            pltpu.VMEM((4,) + chunk, BF), pltpu.VMEM((32, 8, WIDE), BF), pltpu.VMEM((32, 8, WIDE), BF),
            pltpu.VMEM(chunk, BF), pltpu.VMEM(chunk, BF), pltpu.VMEM(chunk, BF), pltpu.VMEM(chunk, BF),
            dma((6,)), dma((3,)), dma((3,)), dma((3,)), dma((3,)),
            dma, dma((8,)), dma((3, 8)), dma((3, 8)), dma((6,)), dma((6,)), dma, dma((8,)), dma,
        ],
        compiler_params=pltpu.CompilerParams(
            collective_id=1, has_side_effects=True, vmem_limit_bytes=56 << 20
        ),
        name="layer",
    )(att, wo, residual, gain, logits, routes, placement, wg, wu, wd)


def shifted(value, axis, steps):
    count = lax.axis_size(axis)
    initial, last = (max(0, -steps), min(count, count - steps))
    return lax.ppermute(value, axis, [(source, source + steps) for source in range(initial, last)])


def step_back(keys_in_block, values_in_block):
    return shifted((keys_in_block, values_in_block), "req", 1)


def per_device(
    residual, queries, rotated_key_rows, values, req_start, head_sink_logit, out_proj, mid_gain,
    router_logits, routes, placement, w_gate, w_up, w_down,
):
    tok_count = residual.shape[0]
    req_size = lax.axis_size("req")
    own_req = lax.axis_index("req")
    query_group_width = QUERY_HEADS // KEY_VALUE_HEADS
    kv_heads = rotated_key_rows.shape[1] // HEAD_SIZE
    shard_queries = queries.reshape(tok_count, kv_heads, query_group_width, HEAD_SIZE)
    local_keys = rotated_key_rows.reshape(tok_count, kv_heads, HEAD_SIZE)
    local_values = values.reshape(tok_count, kv_heads, HEAD_SIZE)
    win_span = min(16, req_size // 2)
    window = win_span * tok_count
    query_pos = own_req * tok_count + jnp.arange(tok_count, dtype=jnp.int32)
    logit_scale_factor = HEAD_SIZE ** (-0.5)

    def attend(carry_state, keys_in_block, values_in_block, key_first):
        running_max, row_total, weighted_value_sum = carry_state
        attention_logits = (
            jnp.einsum(
                "veck,uek->ecvu", shard_queries, keys_in_block, preferred_element_type=jnp.float32
            )
            * logit_scale_factor
        )
        key_pos = key_first + jnp.arange(keys_in_block.shape[0], dtype=jnp.int32)
        visible = (
            (key_pos[None, :] >= req_start[:, None])
            & (key_pos[None, :] <= query_pos[:, None])
            & (query_pos[:, None] - key_pos[None, :] < window)
        )
        attention_logits = jnp.where(visible[None, None], attention_logits, -jnp.inf)
        new_max = jnp.maximum(running_max, jnp.max(attention_logits, axis=-1))
        probs = jnp.exp(attention_logits - new_max[..., None])
        factor = jnp.exp(running_max - new_max)
        row_total = row_total * factor + jnp.sum(probs, axis=-1)
        weighted_value_sum = weighted_value_sum * factor[..., None] + jnp.einsum(
            "plyw,wpj->plyj",
            probs.astype(jnp.bfloat16),
            values_in_block,
            preferred_element_type=jnp.float32,
        )
        return (new_max, row_total, weighted_value_sum)

    initial_sink_logit = jnp.broadcast_to(
        head_sink_logit.reshape(kv_heads, query_group_width, 1),
        (kv_heads, query_group_width, tok_count),
    )
    carry_state = (
        initial_sink_logit,
        jnp.ones((kv_heads, query_group_width, tok_count), jnp.float32),
        jnp.zeros((kv_heads, query_group_width, tok_count, HEAD_SIZE), jnp.float32),
    )
    carry_state = attend(carry_state, local_keys, local_values, own_req * tok_count)

    def pair_step(step_idx, loop_carry):
        folded, near_keys, near_values = loop_carry
        mid_keys, mid_values = step_back(near_keys, near_values)
        far_keys, far_values = step_back(mid_keys, mid_values)
        key_first = (own_req - 2 * step_idx - 2) * tok_count
        folded = attend(
            folded,
            jnp.concatenate([far_keys, mid_keys], 0),
            jnp.concatenate([far_values, mid_values], 0),
            key_first,
        )
        return (folded, far_keys, far_values)

    carry_state, unused_keys, unused_values = lax.fori_loop(
        0, win_span // 2, pair_step, (carry_state, local_keys, local_values)
    )
    running_max, row_total, weighted_value_sum = carry_state
    attended = (weighted_value_sum / row_total[..., None]).astype(jnp.bfloat16)
    flat_attended = jnp.transpose(attended, (2, 0, 1, 3)).reshape(tok_count, -1)
    wo = lax.all_gather(out_proj.T, "req", axis=0, tiled=True)
    return layer_call(
        flat_attended, wo, residual, mid_gain.reshape(1, D), router_logits.T, routes.T,
        placement.reshape(1, NREQ), w_gate[0], w_up[0], w_down[0],
    )


def solution(mesh):
    in_specs = (
        P("req", None),
        P("req", "ffn"),
        P("req", "ffn"),
        P("req", "ffn"),
        P("req"),
        P("ffn"),
        P("ffn", "req"),
        P(),
        P("req", None),
        P("req", None),
        P(),
        P("req", None, "ffn"),
        P("req", None, "ffn"),
        P("req", None, "ffn"),
    )
    out_specs = P("req", "ffn")
    return jax.shard_map(
        per_device, mesh=mesh, in_specs=in_specs, out_specs=out_specs, check_vma=False
    )
```

time: 696 us -> 356 us (0.51); the launches traced: 686 us -> 354 us
  blocking collectives: 209 us -> 0 us
  Pallas kernels: 0 us -> 133 us
  waiting for transfers between devices: 189 us -> 81.2 us
  local copies, waits for them, and re-layouts: 105 us -> 10.3 us
  matrix products: 60.6 us -> 29.1 us
  other arithmetic: 29.8 us -> 10.6 us
    all_to_all x2 -> x0, blocking collectives: 209 us -> none  [the longest x1 108 us: per_device(): lax.all_to_all(send_rows, 'req', split_axis=0, concat_axis=0, tiled=True)]
    pallas_call x0 -> x1, Pallas kernels: none -> 133 us  [layer_call(): pl.pallas_call(layer_kernel, out_shape=jax.ShapeDtypeStruct((TOK, Q), BF)...]
    psum x1 -> x0, waiting for transfers between devices: 74.1 us -> none  [per_device(): summed = lax.psum(proj.astype(jnp.bfloat16), 'ffn').astype(jnp.float32)]
    all_to_all x1 -> x0, waiting for transfers between devices: 30.6 us -> none  [per_device(): lax.all_to_all(lax.all_to_all(partial_rows[None], 'req', split_axis=1, co...]
    all_to_all x2 -> x0, local copies, waits for them, and re-layouts: 22.2 us -> none  [the longest x1 14.3 us: per_device(): lax.all_to_all(partial_rows[None], 'req', split_axis=1, concat_axis=1, ti...]
    dot_general x3 -> x0, matrix products: 20.5 us -> none  [the longest x1 9.66 us: per_device(): lax.dot_general(activated, down_mat, (((1,), (1,)), ((), ())), preferred_...]
    unnamed x31 -> x9, local copies, waits for them, and re-layouts: 25.2 us -> 7.79 us
    reshape x4 -> x1, local copies, waits for them, and re-layouts: 15 us -> 1.17 us  [per_device(): flat_attended = jnp.transpose(attended, (2, 0, 1, 3)).reshape(tok_count, -1)]
  transfers between devices with their start and end apart: 35 -> 33, of which waited for: 19 -> 18; matrix products, arithmetic and copies ran while one was open for 10% -> 14% of each run, Pallas kernels for 0% -> 0%
where the time goes in v1:
time: 356 us; the launch traced here: 354 us
  Pallas kernels  133 us (37%)
  waiting for transfers between devices  81.2 us (23%)
  starting transfers between devices  74.9 us (21%)
  matrix products  29.1 us (8%)
  between operations  13.5 us (4%)
  other arithmetic  10.6 us (3%)
  local copies, waits for them, and re-layouts  10.3 us (3%)
    pallas_call x1, Pallas kernels, layer_call(): pl.pallas_call(layer_kernel, out_shape=jax.ShapeDtypeStruct((TOK, Q), BF)...  133 us
    ppermute x32, waiting for transfers between devices, shifted(): lax.ppermute(value, axis, [(source, source + steps) for source in range(i...  80.5 us
    ppermute x32, starting transfers between devices, shifted(): lax.ppermute(value, axis, [(source, source + steps) for source in range(i...  74.9 us
    dot_general x9, matrix products, attend(): jnp.einsum('veck,uek->ecvu', shard_queries, keys_in_block, preferred_elem...  15.6 us
    dot_general x9, matrix products, attend(): jnp.einsum('plyw,wpj->plyj', probs.astype(jnp.bfloat16), values_in_block,...  13.5 us
    unnamed x9, local copies, waits for them, and re-layouts  7.79 us
    reduce_sum x9, other arithmetic, attend(): row_total = row_total * factor + jnp.sum(probs, axis=-1)  7.31 us
  transfers between devices with their start and end apart: 33, of which 18 were waited for; matrix products, arithmetic and copies ran while one was open for 14% of the time, Pallas kernels for 0%

profile of v1, /device:TPU:33, one launch (start us, length us, event | category | flops | bytes accessed | tf_op | source)
XLA Modules:
  0.0 353.5 jit_solution(13188832130858068245)
XLA Ops:
  16.8 193.3 %while.24 = (s32[]{:T(128)}, f32[4,2,256]{2,1,0:T(2,128)S(1)}, f32[4,2,256]{2,1,0:T(2,128)S(1)}, f32[4,2,256,128]{3,2,1,0:T(8,128)S(1)}, bf16[256,4,128]{2,0,1:T...) while((s32[]{:T(128)}, f32[4,2,256]{2,1,0:T(2,128)S(1)}, ...), condition=%wide.region_5.6_spmd.clone, body=%wide.region_2.5_spmd.clone.sunk | while | flops 551817984 | bytes 23207316 | solution.py:401
  16.8 3.7 %collective-permute-start = (bf16[256,4,128]{2,0,1:T(8,128)(2,1)}, bf16[256,4,128]{2,0,1:T(8,128)(2,1)S(1)}, u32[]{:S(2)}, u32[]{:S(2)}) collective-permute-start(bf16[256,4,128]{2,0,1:T(8,128)(2,1)} %get-tuple-element.402), channel_id=1, source_target_pairs={{0,4},{4,8},{8,12},{12,16},{16,20},{20,24},{24,28},{28,32},{32,36}... | collective-permute-start | bytes 786440 | tf_op jit(solution)/shard_map/while/body/eval_jaxpr/ppermute | solution.py:326
  20.5 1.9 collective-permute-start.2
  24.1 4.3 %collective-permute-start.1 = (bf16[256,4,128]{2,0,1:T(8,128)(2,1)S(1)}, bf16[256,4,128]{2,0,1:T(8,128)(2,1)S(1)}, u32[]{:S(2)}, u32[]{:S(2)}) collective-permute-start(bf16[256,4,128]{2,0,1:T(8,128)(2,1)S(1)} %collective-permute-done), channel_id=1, source_target_pairs={{0,4},{4,8},{8,12},{12,16},{16,20},{20,24},{24,28},{28,32},{32,36}... | collective-permute-start | bytes 786440 | tf_op jit(solution)/shard_map/while/body/eval_jaxpr/ppermute | solution.py:326
  28.6 2.9 collective-permute-start.3
  36.5 4.4 %collective-permute-start = (bf16[256,4,128]{2,0,1:T(8,128)(2,1)}, bf16[256,4,128]{2,0,1:T(8,128)(2,1)S(1)}, u32[]{:S(2)}, u32[]{:S(2)}) collective-permute-start(bf16[256,4,128]{2,0,1:T(8,128)(2,1)} %get-tuple-element.402), channel_id=1, source_target_pairs={{0,4},{4,8},{8,12},{12,16},{16,20},{20,24},{24,28},{28,32},{32,36}... | collective-permute-start | bytes 786440 | tf_op jit(solution)/shard_map/while/body/eval_jaxpr/ppermute | solution.py:326
  40.9 1.9 collective-permute-start.2
  42.9 2.7 collective-permute-done
  45.6 3.2 collective-permute-start.1
  49.0 2.6 collective-permute-start.3
  51.6 3.8 %collective-permute-done.1 = bf16[256,4,128]{2,0,1:T(8,128)(2,1)S(1)} collective-permute-done((bf16[256,4,128]{2,0,1:T(8,128)(2,1)S(1)}, bf16[256,4,128]{2,0,1:T(8,128)(2,1)S(1)}, u32[]{:S(2)}, u32[]{:S(2)}) %collective-permute-start.1) | collective-permute-done | bytes 262176 | tf_op jit(solution)/shard_map/while/body/eval_jaxpr/ppermute | solution.py:326
  63.8 6.1 %collective-permute-done = bf16[256,4,128]{2,0,1:T(8,128)(2,1)S(1)} collective-permute-done((bf16[256,4,128]{2,0,1:T(8,128)(2,1)}, bf16[256,4,128]{2,0,1:T(8,128)(2,1)S(1)}, u32[]{:S(2)}, u32[]{:S(2)}) %collective-permute-start) | collective-permute-done | bytes 262176 | tf_op jit(solution)/shard_map/while/body/eval_jaxpr/ppermute | solution.py:326
  70.0 3.9 %collective-permute-start.1 = (bf16[256,4,128]{2,0,1:T(8,128)(2,1)S(1)}, bf16[256,4,128]{2,0,1:T(8,128)(2,1)S(1)}, u32[]{:S(2)}, u32[]{:S(2)}) collective-permute-start(bf16[256,4,128]{2,0,1:T(8,128)(2,1)S(1)} %collective-permute-done), channel_id=1, source_target_pairs={{0,4},{4,8},{8,12},{12,16},{16,20},{20,24},{24,28},{28,32},{32,36}... | collective-permute-start | bytes 786440 | tf_op jit(solution)/shard_map/while/body/eval_jaxpr/ppermute | solution.py:326
  74.1 4.0 %collective-permute-start.3 = (bf16[256,4,128]{2,0,1:T(8,128)(2,1)S(1)}, bf16[256,4,128]{2,0,1:T(8,128)(2,1)S(1)}, u32[]{:S(2)}, u32[]{:S(2)}) collective-permute-start(bf16[256,4,128]{2,0,1:T(8,128)(2,1)S(1)} %collective-permute-done.2), channel_id=1, source_target_pairs={{0,4},{4,8},{8,12},{12,16},{16,20},{20,24},{24,28},{28,32},{32,36}... | collective-permute-start | bytes 786440 | tf_op jit(solution)/shard_map/while/body/eval_jaxpr/ppermute | solution.py:326
  78.1 4.0 %collective-permute-done.1 = bf16[256,4,128]{2,0,1:T(8,128)(2,1)S(1)} collective-permute-done((bf16[256,4,128]{2,0,1:T(8,128)(2,1)S(1)}, bf16[256,4,128]{2,0,1:T(8,128)(2,1)S(1)}, u32[]{:S(2)}, u32[]{:S(2)}) %collective-permute-start.1) | collective-permute-done | bytes 262176 | tf_op jit(solution)/shard_map/while/body/eval_jaxpr/ppermute | solution.py:326
  84.9 2.4 collective-permute-done.3
  92.8 6.1 %collective-permute-done = bf16[256,4,128]{2,0,1:T(8,128)(2,1)S(1)} collective-permute-done((bf16[256,4,128]{2,0,1:T(8,128)(2,1)}, bf16[256,4,128]{2,0,1:T(8,128)(2,1)S(1)}, u32[]{:S(2)}, u32[]{:S(2)}) %collective-permute-start) | collective-permute-done | bytes 262176 | tf_op jit(solution)/shard_map/while/body/eval_jaxpr/ppermute | solution.py:326
  101.1 1.9 collective-permute-start.3
  103.0 5.7 %collective-permute-done.1 = bf16[256,4,128]{2,0,1:T(8,128)(2,1)S(1)} collective-permute-done((bf16[256,4,128]{2,0,1:T(8,128)(2,1)S(1)}, bf16[256,4,128]{2,0,1:T(8,128)(2,1)S(1)}, u32[]{:S(2)}, u32[]{:S(2)}) %collective-permute-start.1) | collective-permute-done | bytes 262176 | tf_op jit(solution)/shard_map/while/body/eval_jaxpr/ppermute | solution.py:326
  117.0 6.1 %collective-permute-done = bf16[256,4,128]{2,0,1:T(8,128)(2,1)S(1)} collective-permute-done((bf16[256,4,128]{2,0,1:T(8,128)(2,1)}, bf16[256,4,128]{2,0,1:T(8,128)(2,1)S(1)}, u32[]{:S(2)}, u32[]{:S(2)}) %collective-permute-start) | collective-permute-done | bytes 262176 | tf_op jit(solution)/shard_map/while/body/eval_jaxpr/ppermute | solution.py:326
  125.3 1.9 collective-permute-start.3
  127.2 5.7 %collective-permute-done.1 = bf16[256,4,128]{2,0,1:T(8,128)(2,1)S(1)} collective-permute-done((bf16[256,4,128]{2,0,1:T(8,128)(2,1)S(1)}, bf16[256,4,128]{2,0,1:T(8,128)(2,1)S(1)}, u32[]{:S(2)}, u32[]{:S(2)}) %collective-permute-start.1) | collective-permute-done | bytes 262176 | tf_op jit(solution)/shard_map/while/body/eval_jaxpr/ppermute | solution.py:326
  141.3 6.1 %collective-permute-done = bf16[256,4,128]{2,0,1:T(8,128)(2,1)S(1)} collective-permute-done((bf16[256,4,128]{2,0,1:T(8,128)(2,1)}, bf16[256,4,128]{2,0,1:T(8,128)(2,1)S(1)}, u32[]{:S(2)}, u32[]{:S(2)}) %collective-permute-start) | collective-permute-done | bytes 262176 | tf_op jit(solution)/shard_map/while/body/eval_jaxpr/ppermute | solution.py:326
  149.6 1.9 collective-permute-start.3
  151.5 5.7 %collective-permute-done.1 = bf16[256,4,128]{2,0,1:T(8,128)(2,1)S(1)} collective-permute-done((bf16[256,4,128]{2,0,1:T(8,128)(2,1)S(1)}, bf16[256,4,128]{2,0,1:T(8,128)(2,1)S(1)}, u32[]{:S(2)}, u32[]{:S(2)}) %collective-permute-start.1) | collective-permute-done | bytes 262176 | tf_op jit(solution)/shard_map/while/body/eval_jaxpr/ppermute | solution.py:326
  165.5 6.1 %collective-permute-done = bf16[256,4,128]{2,0,1:T(8,128)(2,1)S(1)} collective-permute-done((bf16[256,4,128]{2,0,1:T(8,128)(2,1)}, bf16[256,4,128]{2,0,1:T(8,128)(2,1)S(1)}, u32[]{:S(2)}, u32[]{:S(2)}) %collective-permute-start) | collective-permute-done | bytes 262176 | tf_op jit(solution)/shard_map/while/body/eval_jaxpr/ppermute | solution.py:326
  173.8 1.9 collective-permute-start.3
  175.8 5.7 %collective-permute-done.1 = bf16[256,4,128]{2,0,1:T(8,128)(2,1)S(1)} collective-permute-done((bf16[256,4,128]{2,0,1:T(8,128)(2,1)S(1)}, bf16[256,4,128]{2,0,1:T(8,128)(2,1)S(1)}, u32[]{:S(2)}, u32[]{:S(2)}) %collective-permute-start.1) | collective-permute-done | bytes 262176 | tf_op jit(solution)/shard_map/while/body/eval_jaxpr/ppermute | solution.py:326
  189.8 6.1 %collective-permute-done = bf16[256,4,128]{2,0,1:T(8,128)(2,1)S(1)} collective-permute-done((bf16[256,4,128]{2,0,1:T(8,128)(2,1)}, bf16[256,4,128]{2,0,1:T(8,128)(2,1)S(1)}, u32[]{:S(2)}, u32[]{:S(2)}) %collective-permute-start) | collective-permute-done | bytes 262176 | tf_op jit(solution)/shard_map/while/body/eval_jaxpr/ppermute | solution.py:326
  198.1 1.9 collective-permute-start.3
  200.0 5.7 %collective-permute-done.1 = bf16[256,4,128]{2,0,1:T(8,128)(2,1)S(1)} collective-permute-done((bf16[256,4,128]{2,0,1:T(8,128)(2,1)S(1)}, bf16[256,4,128]{2,0,1:T(8,128)(2,1)S(1)}, u32[]{:S(2)}, u32[]{:S(2)}) %collective-permute-start.1) | collective-permute-done | bytes 262176 | tf_op jit(solution)/shard_map/while/body/eval_jaxpr/ppermute | solution.py:326
  212.2 132.8 %layer.1 = bf16[256,512]{1,0:T(8,128)(2,1)} custom-call(bf16[256,1024]{1,0:T(8,128)(2,1)} %reshape.216.att_ref, bf16[2048,1024]{1,0:T(8,128)(2,1)} %all-gather.2.cloned.1.call-done.wo_hbm, bf16[256,2048]{1,0:T(8,128)(2,1)} %res_hbm.1, f32[1,2048]{1,0:T(1,128)} %bitcast.96, f32[8,256]{1,0:T(8,128)} %bitcast.97, s32[2,256]{1,0:T(2,128)} %bitcast.98, ...), custom_call_target="tpu_custom_call" | custom-call | tf_op jit(solution)/shard_map/layer/pallas_call | solution.py:298
  (161 shorter events, 85.6 us)
Async XLA Ops:
  6.5 205.7 %all-gather.2.cloned.1.call-start = ((), (), s32[]{:S(2)}) async-start(), calls=%async_computation | async-start | bytes 4259840 | tf_op jit(solution)/shard_map/all_gather | solution.py:407
  16.8 7.3 %collective-permute-start = (bf16[256,4,128]{2,0,1:T(8,128)(2,1)}, bf16[256,4,128]{2,0,1:T(8,128)(2,1)S(1)}, u32[]{:S(2)}, u32[]{:S(2)}) collective-permute-start(bf16[256,4,128]{2,0,1:T(8,128)(2,1)} %get-tuple-element.402), channel_id=1, source_target_pairs={{0,4},{4,8},{8,12},{12,16},{16,20},{20,24},{24,28},{28,32},{32,36}... | collective-permute-start | bytes 786440 | tf_op jit(solution)/shard_map/while/body/eval_jaxpr/ppermute | solution.py:326
  20.5 8.1 %collective-permute-start.2 = (bf16[256,4,128]{2,0,1:T(8,128)(2,1)}, bf16[256,4,128]{2,0,1:T(8,128)(2,1)S(1)}, u32[]{:S(2)}, u32[]{:S(2)}) collective-permute-start(bf16[256,4,128]{2,0,1:T(8,128)(2,1)} %get-tuple-element.403), channel_id=1, source_target_pairs={{0,4},{4,8},{8,12},{12,16},{16,20},{20,24},{24,28},{28,32},{32,36}... | collective-permute-start | bytes 786440 | tf_op jit(solution)/shard_map/while/body/eval_jaxpr/ppermute | solution.py:326
  24.1 7.9 %collective-permute-start.1 = (bf16[256,4,128]{2,0,1:T(8,128)(2,1)S(1)}, bf16[256,4,128]{2,0,1:T(8,128)(2,1)S(1)}, u32[]{:S(2)}, u32[]{:S(2)}) collective-permute-start(bf16[256,4,128]{2,0,1:T(8,128)(2,1)S(1)} %collective-permute-done), channel_id=1, source_target_pairs={{0,4},{4,8},{8,12},{12,16},{16,20},{20,24},{24,28},{28,32},{32,36}... | collective-permute-start | bytes 786440 | tf_op jit(solution)/shard_map/while/body/eval_jaxpr/ppermute | solution.py:326
  36.5 9.1 %collective-permute-start = (bf16[256,4,128]{2,0,1:T(8,128)(2,1)}, bf16[256,4,128]{2,0,1:T(8,128)(2,1)S(1)}, u32[]{:S(2)}, u32[]{:S(2)}) collective-permute-start(bf16[256,4,128]{2,0,1:T(8,128)(2,1)} %get-tuple-element.402), channel_id=1, source_target_pairs={{0,4},{4,8},{8,12},{12,16},{16,20},{20,24},{24,28},{28,32},{32,36}... | collective-permute-start | bytes 786440 | tf_op jit(solution)/shard_map/while/body/eval_jaxpr/ppermute | solution.py:326
  40.9 8.1 %collective-permute-start.2 = (bf16[256,4,128]{2,0,1:T(8,128)(2,1)}, bf16[256,4,128]{2,0,1:T(8,128)(2,1)S(1)}, u32[]{:S(2)}, u32[]{:S(2)}) collective-permute-start(bf16[256,4,128]{2,0,1:T(8,128)(2,1)} %get-tuple-element.403), channel_id=1, source_target_pairs={{0,4},{4,8},{8,12},{12,16},{16,20},{20,24},{24,28},{28,32},{32,36}... | collective-permute-start | bytes 786440 | tf_op jit(solution)/shard_map/while/body/eval_jaxpr/ppermute | solution.py:326
  45.6 9.9 %collective-permute-start.1 = (bf16[256,4,128]{2,0,1:T(8,128)(2,1)S(1)}, bf16[256,4,128]{2,0,1:T(8,128)(2,1)S(1)}, u32[]{:S(2)}, u32[]{:S(2)}) collective-permute-start(bf16[256,4,128]{2,0,1:T(8,128)(2,1)S(1)} %collective-permute-done), channel_id=1, source_target_pairs={{0,4},{4,8},{8,12},{12,16},{16,20},{20,24},{24,28},{28,32},{32,36}... | collective-permute-start | bytes 786440 | tf_op jit(solution)/shard_map/while/body/eval_jaxpr/ppermute | solution.py:326
  49.0 9.3 %collective-permute-start.3 = (bf16[256,4,128]{2,0,1:T(8,128)(2,1)S(1)}, bf16[256,4,128]{2,0,1:T(8,128)(2,1)S(1)}, u32[]{:S(2)}, u32[]{:S(2)}) collective-permute-start(bf16[256,4,128]{2,0,1:T(8,128)(2,1)S(1)} %collective-permute-done.2), channel_id=1, source_target_pairs={{0,4},{4,8},{8,12},{12,16},{16,20},{20,24},{24,28},{28,32},{32,36}... | collective-permute-start | bytes 786440 | tf_op jit(solution)/shard_map/while/body/eval_jaxpr/ppermute | solution.py:326
  60.0 10.0 %collective-permute-start = (bf16[256,4,128]{2,0,1:T(8,128)(2,1)}, bf16[256,4,128]{2,0,1:T(8,128)(2,1)S(1)}, u32[]{:S(2)}, u32[]{:S(2)}) collective-permute-start(bf16[256,4,128]{2,0,1:T(8,128)(2,1)} %get-tuple-element.402), channel_id=1, source_target_pairs={{0,4},{4,8},{8,12},{12,16},{16,20},{20,24},{24,28},{28,32},{32,36}... | collective-permute-start | bytes 786440 | tf_op jit(solution)/shard_map/while/body/eval_jaxpr/ppermute | solution.py:326
  61.9 12.2 %collective-permute-start.2 = (bf16[256,4,128]{2,0,1:T(8,128)(2,1)}, bf16[256,4,128]{2,0,1:T(8,128)(2,1)S(1)}, u32[]{:S(2)}, u32[]{:S(2)}) collective-permute-start(bf16[256,4,128]{2,0,1:T(8,128)(2,1)} %get-tuple-element.403), channel_id=1, source_target_pairs={{0,4},{4,8},{8,12},{12,16},{16,20},{20,24},{24,28},{28,32},{32,36}... | collective-permute-start | bytes 786440 | tf_op jit(solution)/shard_map/while/body/eval_jaxpr/ppermute | solution.py:326
  70.0 12.1 %collective-permute-start.1 = (bf16[256,4,128]{2,0,1:T(8,128)(2,1)S(1)}, bf16[256,4,128]{2,0,1:T(8,128)(2,1)S(1)}, u32[]{:S(2)}, u32[]{:S(2)}) collective-permute-start(bf16[256,4,128]{2,0,1:T(8,128)(2,1)S(1)} %collective-permute-done), channel_id=1, source_target_pairs={{0,4},{4,8},{8,12},{12,16},{16,20},{20,24},{24,28},{28,32},{32,36}... | collective-permute-start | bytes 786440 | tf_op jit(solution)/shard_map/while/body/eval_jaxpr/ppermute | solution.py:326
  74.1 13.2 %collective-permute-start.3 = (bf16[256,4,128]{2,0,1:T(8,128)(2,1)S(1)}, bf16[256,4,128]{2,0,1:T(8,128)(2,1)S(1)}, u32[]{:S(2)}, u32[]{:S(2)}) collective-permute-start(bf16[256,4,128]{2,0,1:T(8,128)(2,1)S(1)} %collective-permute-done.2), channel_id=1, source_target_pairs={{0,4},{4,8},{8,12},{12,16},{16,20},{20,24},{24,28},{28,32},{32,36}... | collective-permute-start | bytes 786440 | tf_op jit(solution)/shard_map/while/body/eval_jaxpr/ppermute | solution.py:326
  88.9 10.0 %collective-permute-start = (bf16[256,4,128]{2,0,1:T(8,128)(2,1)}, bf16[256,4,128]{2,0,1:T(8,128)(2,1)S(1)}, u32[]{:S(2)}, u32[]{:S(2)}) collective-permute-start(bf16[256,4,128]{2,0,1:T(8,128)(2,1)} %get-tuple-element.402), channel_id=1, source_target_pairs={{0,4},{4,8},{8,12},{12,16},{16,20},{20,24},{24,28},{28,32},{32,36}... | collective-permute-start | bytes 786440 | tf_op jit(solution)/shard_map/while/body/eval_jaxpr/ppermute | solution.py:326
  90.8 10.2 %collective-permute-start.2 = (bf16[256,4,128]{2,0,1:T(8,128)(2,1)}, bf16[256,4,128]{2,0,1:T(8,128)(2,1)S(1)}, u32[]{:S(2)}, u32[]{:S(2)}) collective-permute-start(bf16[256,4,128]{2,0,1:T(8,128)(2,1)} %get-tuple-element.403), channel_id=1, source_target_pairs={{0,4},{4,8},{8,12},{12,16},{16,20},{20,24},{24,28},{28,32},{32,36}... | collective-permute-start | bytes 786440 | tf_op jit(solution)/shard_map/while/body/eval_jaxpr/ppermute | solution.py:326
  98.9 9.8 %collective-permute-start.1 = (bf16[256,4,128]{2,0,1:T(8,128)(2,1)S(1)}, bf16[256,4,128]{2,0,1:T(8,128)(2,1)S(1)}, u32[]{:S(2)}, u32[]{:S(2)}) collective-permute-start(bf16[256,4,128]{2,0,1:T(8,128)(2,1)S(1)} %collective-permute-done), channel_id=1, source_target_pairs={{0,4},{4,8},{8,12},{12,16},{16,20},{20,24},{24,28},{28,32},{32,36}... | collective-permute-start | bytes 786440 | tf_op jit(solution)/shard_map/while/body/eval_jaxpr/ppermute | solution.py:326
  101.1 10.4 %collective-permute-start.3 = (bf16[256,4,128]{2,0,1:T(8,128)(2,1)S(1)}, bf16[256,4,128]{2,0,1:T(8,128)(2,1)S(1)}, u32[]{:S(2)}, u32[]{:S(2)}) collective-permute-start(bf16[256,4,128]{2,0,1:T(8,128)(2,1)S(1)} %collective-permute-done.2), channel_id=1, source_target_pairs={{0,4},{4,8},{8,12},{12,16},{16,20},{20,24},{24,28},{28,32},{32,36}... | collective-permute-start | bytes 786440 | tf_op jit(solution)/shard_map/while/body/eval_jaxpr/ppermute | solution.py:326
  113.1 10.0 %collective-permute-start = (bf16[256,4,128]{2,0,1:T(8,128)(2,1)}, bf16[256,4,128]{2,0,1:T(8,128)(2,1)S(1)}, u32[]{:S(2)}, u32[]{:S(2)}) collective-permute-start(bf16[256,4,128]{2,0,1:T(8,128)(2,1)} %get-tuple-element.402), channel_id=1, source_target_pairs={{0,4},{4,8},{8,12},{12,16},{16,20},{20,24},{24,28},{28,32},{32,36}... | collective-permute-start | bytes 786440 | tf_op jit(solution)/shard_map/while/body/eval_jaxpr/ppermute | solution.py:326
  115.1 10.2 %collective-permute-start.2 = (bf16[256,4,128]{2,0,1:T(8,128)(2,1)}, bf16[256,4,128]{2,0,1:T(8,128)(2,1)S(1)}, u32[]{:S(2)}, u32[]{:S(2)}) collective-permute-start(bf16[256,4,128]{2,0,1:T(8,128)(2,1)} %get-tuple-element.403), channel_id=1, source_target_pairs={{0,4},{4,8},{8,12},{12,16},{16,20},{20,24},{24,28},{28,32},{32,36}... | collective-permute-start | bytes 786440 | tf_op jit(solution)/shard_map/while/body/eval_jaxpr/ppermute | solution.py:326
  123.1 9.8 %collective-permute-start.1 = (bf16[256,4,128]{2,0,1:T(8,128)(2,1)S(1)}, bf16[256,4,128]{2,0,1:T(8,128)(2,1)S(1)}, u32[]{:S(2)}, u32[]{:S(2)}) collective-permute-start(bf16[256,4,128]{2,0,1:T(8,128)(2,1)S(1)} %collective-permute-done), channel_id=1, source_target_pairs={{0,4},{4,8},{8,12},{12,16},{16,20},{20,24},{24,28},{28,32},{32,36}... | collective-permute-start | bytes 786440 | tf_op jit(solution)/shard_map/while/body/eval_jaxpr/ppermute | solution.py:326
  125.3 10.4 %collective-permute-start.3 = (bf16[256,4,128]{2,0,1:T(8,128)(2,1)S(1)}, bf16[256,4,128]{2,0,1:T(8,128)(2,1)S(1)}, u32[]{:S(2)}, u32[]{:S(2)}) collective-permute-start(bf16[256,4,128]{2,0,1:T(8,128)(2,1)S(1)} %collective-permute-done.2), channel_id=1, source_target_pairs={{0,4},{4,8},{8,12},{12,16},{16,20},{20,24},{24,28},{28,32},{32,36}... | collective-permute-start | bytes 786440 | tf_op jit(solution)/shard_map/while/body/eval_jaxpr/ppermute | solution.py:326
  137.4 10.0 %collective-permute-start = (bf16[256,4,128]{2,0,1:T(8,128)(2,1)}, bf16[256,4,128]{2,0,1:T(8,128)(2,1)S(1)}, u32[]{:S(2)}, u32[]{:S(2)}) collective-permute-start(bf16[256,4,128]{2,0,1:T(8,128)(2,1)} %get-tuple-element.402), channel_id=1, source_target_pairs={{0,4},{4,8},{8,12},{12,16},{16,20},{20,24},{24,28},{28,32},{32,36}... | collective-permute-start | bytes 786440 | tf_op jit(solution)/shard_map/while/body/eval_jaxpr/ppermute | solution.py:326
  139.3 10.2 %collective-permute-start.2 = (bf16[256,4,128]{2,0,1:T(8,128)(2,1)}, bf16[256,4,128]{2,0,1:T(8,128)(2,1)S(1)}, u32[]{:S(2)}, u32[]{:S(2)}) collective-permute-start(bf16[256,4,128]{2,0,1:T(8,128)(2,1)} %get-tuple-element.403), channel_id=1, source_target_pairs={{0,4},{4,8},{8,12},{12,16},{16,20},{20,24},{24,28},{28,32},{32,36}... | collective-permute-start | bytes 786440 | tf_op jit(solution)/shard_map/while/body/eval_jaxpr/ppermute | solution.py:326
  147.4 9.8 %collective-permute-start.1 = (bf16[256,4,128]{2,0,1:T(8,128)(2,1)S(1)}, bf16[256,4,128]{2,0,1:T(8,128)(2,1)S(1)}, u32[]{:S(2)}, u32[]{:S(2)}) collective-permute-start(bf16[256,4,128]{2,0,1:T(8,128)(2,1)S(1)} %collective-permute-done), channel_id=1, source_target_pairs={{0,4},{4,8},{8,12},{12,16},{16,20},{20,24},{24,28},{28,32},{32,36}... | collective-permute-start | bytes 786440 | tf_op jit(solution)/shard_map/while/body/eval_jaxpr/ppermute | solution.py:326
  149.6 10.4 %collective-permute-start.3 = (bf16[256,4,128]{2,0,1:T(8,128)(2,1)S(1)}, bf16[256,4,128]{2,0,1:T(8,128)(2,1)S(1)}, u32[]{:S(2)}, u32[]{:S(2)}) collective-permute-start(bf16[256,4,128]{2,0,1:T(8,128)(2,1)S(1)} %collective-permute-done.2), channel_id=1, source_target_pairs={{0,4},{4,8},{8,12},{12,16},{16,20},{20,24},{24,28},{28,32},{32,36}... | collective-permute-start | bytes 786440 | tf_op jit(solution)/shard_map/while/body/eval_jaxpr/ppermute | solution.py:326
  161.6 10.0 %collective-permute-start = (bf16[256,4,128]{2,0,1:T(8,128)(2,1)}, bf16[256,4,128]{2,0,1:T(8,128)(2,1)S(1)}, u32[]{:S(2)}, u32[]{:S(2)}) collective-permute-start(bf16[256,4,128]{2,0,1:T(8,128)(2,1)} %get-tuple-element.402), channel_id=1, source_target_pairs={{0,4},{4,8},{8,12},{12,16},{16,20},{20,24},{24,28},{28,32},{32,36}... | collective-permute-start | bytes 786440 | tf_op jit(solution)/shard_map/while/body/eval_jaxpr/ppermute | solution.py:326
  163.6 10.2 %collective-permute-start.2 = (bf16[256,4,128]{2,0,1:T(8,128)(2,1)}, bf16[256,4,128]{2,0,1:T(8,128)(2,1)S(1)}, u32[]{:S(2)}, u32[]{:S(2)}) collective-permute-start(bf16[256,4,128]{2,0,1:T(8,128)(2,1)} %get-tuple-element.403), channel_id=1, source_target_pairs={{0,4},{4,8},{8,12},{12,16},{16,20},{20,24},{24,28},{28,32},{32,36}... | collective-permute-start | bytes 786440 | tf_op jit(solution)/shard_map/while/body/eval_jaxpr/ppermute | solution.py:326
  171.7 9.8 %collective-permute-start.1 = (bf16[256,4,128]{2,0,1:T(8,128)(2,1)S(1)}, bf16[256,4,128]{2,0,1:T(8,128)(2,1)S(1)}, u32[]{:S(2)}, u32[]{:S(2)}) collective-permute-start(bf16[256,4,128]{2,0,1:T(8,128)(2,1)S(1)} %collective-permute-done), channel_id=1, source_target_pairs={{0,4},{4,8},{8,12},{12,16},{16,20},{20,24},{24,28},{28,32},{32,36}... | collective-permute-start | bytes 786440 | tf_op jit(solution)/shard_map/while/body/eval_jaxpr/ppermute | solution.py:326
  173.8 10.4 %collective-permute-start.3 = (bf16[256,4,128]{2,0,1:T(8,128)(2,1)S(1)}, bf16[256,4,128]{2,0,1:T(8,128)(2,1)S(1)}, u32[]{:S(2)}, u32[]{:S(2)}) collective-permute-start(bf16[256,4,128]{2,0,1:T(8,128)(2,1)S(1)} %collective-permute-done.2), channel_id=1, source_target_pairs={{0,4},{4,8},{8,12},{12,16},{16,20},{20,24},{24,28},{28,32},{32,36}... | collective-permute-start | bytes 786440 | tf_op jit(solution)/shard_map/while/body/eval_jaxpr/ppermute | solution.py:326
  185.9 10.0 %collective-permute-start = (bf16[256,4,128]{2,0,1:T(8,128)(2,1)}, bf16[256,4,128]{2,0,1:T(8,128)(2,1)S(1)}, u32[]{:S(2)}, u32[]{:S(2)}) collective-permute-start(bf16[256,4,128]{2,0,1:T(8,128)(2,1)} %get-tuple-element.402), channel_id=1, source_target_pairs={{0,4},{4,8},{8,12},{12,16},{16,20},{20,24},{24,28},{28,32},{32,36}... | collective-permute-start | bytes 786440 | tf_op jit(solution)/shard_map/while/body/eval_jaxpr/ppermute | solution.py:326
  187.8 10.2 %collective-permute-start.2 = (bf16[256,4,128]{2,0,1:T(8,128)(2,1)}, bf16[256,4,128]{2,0,1:T(8,128)(2,1)S(1)}, u32[]{:S(2)}, u32[]{:S(2)}) collective-permute-start(bf16[256,4,128]{2,0,1:T(8,128)(2,1)} %get-tuple-element.403), channel_id=1, source_target_pairs={{0,4},{4,8},{8,12},{12,16},{16,20},{20,24},{24,28},{28,32},{32,36}... | collective-permute-start | bytes 786440 | tf_op jit(solution)/shard_map/while/body/eval_jaxpr/ppermute | solution.py:326
  195.9 9.8 %collective-permute-start.1 = (bf16[256,4,128]{2,0,1:T(8,128)(2,1)S(1)}, bf16[256,4,128]{2,0,1:T(8,128)(2,1)S(1)}, u32[]{:S(2)}, u32[]{:S(2)}) collective-permute-start(bf16[256,4,128]{2,0,1:T(8,128)(2,1)S(1)} %collective-permute-done), channel_id=1, source_target_pairs={{0,4},{4,8},{8,12},{12,16},{16,20},{20,24},{24,28},{28,32},{32,36}... | collective-permute-start | bytes 786440 | tf_op jit(solution)/shard_map/while/body/eval_jaxpr/ppermute | solution.py:326
  198.1 10.4 %collective-permute-start.3 = (bf16[256,4,128]{2,0,1:T(8,128)(2,1)S(1)}, bf16[256,4,128]{2,0,1:T(8,128)(2,1)S(1)}, u32[]{:S(2)}, u32[]{:S(2)}) collective-permute-start(bf16[256,4,128]{2,0,1:T(8,128)(2,1)S(1)} %collective-permute-done.2), channel_id=1, source_target_pairs={{0,4},{4,8},{8,12},{12,16},{16,20},{20,24},{24,28},{28,32},{32,36}... | collective-permute-start | bytes 786440 | tf_op jit(solution)/shard_map/while/body/eval_jaxpr/ppermute | solution.py:326
  (18 other events, 45.4 us)
Sparse Core Ops, SparseCore 0:
  10.1 83.4 all-gather.1

commit v2 on v1

--- a/solution.py
+++ b/solution.py
@@ -44,19 +44,31 @@
     )
 
 
+SCALE2 = HEAD_SIZE ** (-0.5) * 1.4426950408889634
+MASKED = -1e30
+
+
 def layer_kernel(
-    att_ref, wo_hbm, res_hbm, gain_hbm, logits_ref, routes_ref, placement_ref, wg_hbm, wu_hbm, wd_hbm,
+    q_hbm, k_hbm, v_hbm, start_hbm, sink_ref, wo_hbm, res_hbm, gain_hbm, logits_ref, routes_ref, placement_ref,
+    wg_hbm, wu_hbm, wd_hbm,
     out_ref,
+    kv, qb, qt, vt, starts, peak, mass, acc, att_out, att_in,
     wo, res, gain, wg, wu, wd,
     proj_send, proj_recv, hid, stat_send, stat_recv,
     e_main, e_rem, g_main, g_rem,
     disp, rows, xbuf, act, part, hop_l, hop_r, from_l, from_r, fin, ret,
+    kv_ssem, kv_rsem, half_ssem, half_rsem, loc_sem, wo_ssem, wo_rsem, ring_ssem, ring_rsem, pair_ssem, pair_rsem,
+    att_ssem, att_rsem,
     in_sem, proj_ssem, proj_rsem, stat_ssem, stat_rsem,
     a2a_ssem, a2a_rsem, ag_ssem, ag_rsem, rs_ssem, rs_rsem, ret_ssem, ret_rsem, own_sem,
 ):
     r = lax.axis_index("req")
     y = lax.axis_index("ffn")
     z = r // 8
+    x = lax.rem(r // 2, 4)
+    c = lax.rem(r, 2)
+    chip = r // 2
+    mate = r + 1 - 2 * c
     yp, ym, y2 = lax.rem(y + 1, 4), lax.rem(y + 3, 4), lax.rem(y + 2, 4)
     peers = (yp, y2, ym)
 
@@ -72,16 +84,188 @@
 
     y_cols = pl.ds(pl.multiple_of(y * Q, Q), Q)
     loads = [
-        pltpu.make_async_copy(wo_hbm, wo, in_sem.at[0]),
-        pltpu.make_async_copy(res_hbm.at[:, y_cols], res, in_sem.at[1]),
-        pltpu.make_async_copy(gain_hbm.at[:, y_cols], gain, in_sem.at[2]),
-        pltpu.make_async_copy(wg_hbm, wg, in_sem.at[3]),
-        pltpu.make_async_copy(wu_hbm, wu, in_sem.at[4]),
-        pltpu.make_async_copy(wd_hbm, wd, in_sem.at[5]),
+        pltpu.make_async_copy(res_hbm.at[:, y_cols], res, in_sem.at[0]),
+        pltpu.make_async_copy(gain_hbm.at[:, y_cols], gain, in_sem.at[1]),
+        pltpu.make_async_copy(wg_hbm, wg, in_sem.at[2]),
+        pltpu.make_async_copy(wu_hbm, wu, in_sem.at[3]),
+        pltpu.make_async_copy(wd_hbm, wd, in_sem.at[4]),
     ]
     for load in loads:
         load.start()
 
+    def head(n):
+        return pl.ds(pl.multiple_of(n * HEAD_SIZE, HEAD_SIZE), HEAD_SIZE)
+
+    own_tok = pl.ds(pl.multiple_of(c * TOK, TOK), TOK)
+    mate_tok = pl.ds(pl.multiple_of((1 - c) * TOK, TOK), TOK)
+    for k in range(2):
+        for i, ref in ((0, k_hbm), (1, v_hbm)):
+            pltpu.make_async_copy(ref.at[:, head(2 * c + k)], kv.at[0, k, i, own_tok], loc_sem.at[k]).start()
+    for k in range(2):
+        for h in range(2):
+            pltpu.make_async_copy(q_hbm.at[:, head(4 * c + 2 * k + h)], qb.at[k, h, own_tok], loc_sem.at[2]).start()
+    pltpu.make_async_copy(start_hbm, starts.at[c], loc_sem.at[3]).start()
+    pltpu.make_async_copy(wo_hbm.at[:, pl.ds(pl.multiple_of(c * 512, 512), 512)], wo.at[c, r], loc_sem.at[4]).start()
+
+    pl.semaphore_wait(bar, NREQ - 1 + 3)
+
+    mate_copies = []
+
+    def to_mate(src, dst, n, sem):
+        copy = remote(src, dst, half_ssem.at[n], sem, mate, y)
+        copy.start()
+        mate_copies.append(copy)
+
+    for k in range(2):
+        for i, ref in ((0, k_hbm), (1, v_hbm)):
+            to_mate(ref.at[:, head(2 * (1 - c) + k)], kv.at[0, k, i, own_tok], 2 * k + i, half_rsem.at[k])
+    for k in range(2):
+        for h in range(2):
+            to_mate(q_hbm.at[:, head(4 * (1 - c) + 2 * k + h)], qb.at[k, h, own_tok], 4 + 2 * k + h, half_rsem.at[2])
+    to_mate(start_hbm, starts.at[c], 8, half_rsem.at[3])
+
+    def chip_at(dz, dx):
+        return lax.rem(z + dz, NZ) * 8 + lax.rem(x + dx, 4) * 2 + c
+
+    def send(src, dst, k, dz, dx):
+        remote(kv.at[src, k], kv.at[dst, k], kv_ssem.at[dst, k], kv_rsem.at[dst, k], chip_at(dz, dx), y).start()
+
+    def took(slot, k):
+        view = kv.at[slot, k]
+        pltpu.make_async_copy(view, view, kv_rsem.at[slot, k]).wait()
+
+    wraps = {1: (x + 1) // 4, 3: (x + 3) // 4}
+    odd = lax.rem(x, 2)
+
+    for k in range(2):
+        view = kv.at[0, k, :, own_tok]
+        pltpu.make_async_copy(view, view, loc_sem.at[k]).wait()
+        view = kv.at[0, k, :, mate_tok]
+        pltpu.make_async_copy(view, view, half_rsem.at[k]).wait()
+        send(0, 4, k, 1, 0)
+        for d in (1, 3):
+            @pl.when(wraps[d] == 0)
+            def _():
+                send(0, d, k, 0, d)
+
+    def took4(k):
+        took(4, k)
+        send(4, 8, k, 1, 0)
+        for d in (1, 3):
+            send(4, d + 4 * (1 - wraps[d]), k, 0, d)
+
+    def took8(k):
+        took(8, k)
+        for d in (1, 3):
+            @pl.when(wraps[d] == 1)
+            def _():
+                send(8, d + 4, k, 0, d)
+
+    def took13(k):
+        took(1, k)
+        took(3, k)
+        send(1 + 2 * odd, 2, k, 0, 1 + 2 * odd)
+
+    def took2(k):
+        took(2, k)
+        send(2, 6, k, 1, 0)
+
+    wo_copies = []
+    for h in range(2):
+        half = pl.ds(h * 512, 512)
+        for dx in range(4):
+            target = z * 8 + lax.rem(x + dx, 4) * 2 + h
+
+            def give(target=target, half=half, h=h):
+                remote(wo_hbm.at[:, half], wo.at[h, r], wo_ssem.at[0], wo_rsem.at[0], target, y).start()
+
+            if dx == 0:
+                pl.when(c != h)(give)
+            else:
+                give()
+
+    def ring(t):
+        g = pl.ds(lax.rem(z + t, NZ) * 8, 8)
+        view = wo.at[c, g]
+        if t == 0:
+            few = wo.at[c, pl.ds(z * 8, 7)]
+            pltpu.make_async_copy(few, few, wo_rsem.at[0]).wait()
+            one = wo.at[c, r]
+            pltpu.make_async_copy(one, one, loc_sem.at[4]).wait()
+        else:
+            pltpu.make_async_copy(view, view, ring_rsem.at[t - 1]).wait()
+        if t < NZ - 1:
+            copy = remote(view, view, ring_ssem.at[t], ring_rsem.at[t], chip_at(NZ - 1, 0), y)
+            copy.start()
+            wo_copies.append(copy)
+        remote(view, view, pair_ssem, pair_rsem, mate, y).start()
+
+    view = qb.at[:, :, own_tok]
+    pltpu.make_async_copy(view, view, loc_sem.at[2]).wait()
+    view = qb.at[:, :, mate_tok]
+    pltpu.make_async_copy(view, view, half_rsem.at[2]).wait()
+    for k in range(2):
+        qt[k] = jnp.concatenate([qb[k, 0].T, qb[k, 1].T], axis=1)
+        for h in range(2):
+            peak[k, :, 512 * h:512 * h + 512] = jnp.full((1, 512), sink_ref[4 * c + 2 * k + h] * HEAD_SIZE ** 0.5, F32)
+    mass[...] = jnp.ones_like(mass)
+    acc[...] = jnp.zeros_like(acc)
+    pltpu.make_async_copy(starts.at[c], starts.at[c], loc_sem.at[3]).wait()
+    pltpu.make_async_copy(starts.at[1 - c], starts.at[1 - c], half_rsem.at[3]).wait()
+    ring(0)
+
+    def attend(s, k):
+        vt[...] = kv[s, k, 1].T
+        first = (chip - s) * 512
+
+        def tiles(h, carry):
+            for half in range(2):
+                cols = pl.ds(pl.multiple_of(h * 512 + half * 256, 256), 256)
+                scores = dot(kv[s, k, 0], qt[k, :, cols])
+                at = iota((1, 256), 1) + 256 * half
+                low = jnp.maximum(starts[half] - first, at + (512 * s - 4095))
+                key = iota((512, 256), 0)
+                seen = key >= low
+                if s == 0:
+                    seen = seen & (key <= at)
+                scores = jnp.where(seen, scores, MASKED)
+                old = peak[k, :, cols]
+                new = jnp.maximum(old, jnp.max(scores, axis=0, keepdims=True))
+                probs = jnp.exp2((scores - new) * SCALE2)
+                alpha = jnp.exp2((old - new) * SCALE2)
+                peak[k, :, cols] = new
+                mass[k, :, cols] = mass[k, :, cols] * alpha + jnp.sum(probs, axis=0, keepdims=True)
+                acc[k, :, cols] = acc[k, :, cols] * alpha + dot(vt[...], probs.astype(BF))
+            return carry
+
+        lax.fori_loop(0, 2, tiles, 0)
+
+    attend(0, 0)
+    took4(0)
+    attend(0, 1)
+    took13(0)
+    ring(1)
+    attend(4, 0)
+    took4(1)
+    attend(1, 0)
+    took13(1)
+    attend(3, 0)
+    ring(2)
+    attend(4, 1)
+    attend(1, 1)
+    took8(0)
+    attend(3, 1)
+    took2(0)
+    ring(3)
+    attend(8, 0)
+    took8(1)
+    attend(2, 0)
+    took2(1)
+    attend(8, 1)
+    ring(4)
+    attend(2, 1)
+    took(5, 0)
+    attend(5, 0)
     route0, route1 = routes_ref[0:1, :], routes_ref[1:2, :]
     dest = iota((NREQ, TOK), 0)
     hot0 = jnp.where(dest == route0, 1.0, 0.0)
@@ -114,12 +298,38 @@
         ref[0] = high
         ref[1] = (gate - high.astype(F32)).astype(BF)
 
-    pl.semaphore_wait(bar, NREQ - 1 + 3)
-
-    loads[0].wait()
+
+    took(7, 0)
+    attend(7, 0)
+    ring(5)
+    took(5, 1)
+    attend(5, 1)
+    took(7, 1)
+    attend(7, 1)
+    ring(6)
+    for k in range(2):
+        took(6, k)
+        attend(6, k)
+    ring(7)
+
+    for k in range(2):
+        out = acc[k] / mass[k]
+        for h in range(2):
+            block = out[:, 512 * h:512 * h + 512].astype(BF).T
+            part_cols = slice(128 * (2 * k + h), 128 * (2 * k + h) + 128)
+            att_out[0, :, part_cols] = block[0:TOK]
+            att_out[1, :, part_cols] = block[TOK:2 * TOK]
+    copy = remote(att_out.at[1 - c], att_in, att_ssem, att_rsem, mate, y)
+    copy.start()
+    mate_copies.append(copy)
+    wo2 = wo.reshape(2, D, 512)
+    pltpu.make_async_copy(wo.at[1 - c], wo.at[1 - c], pair_rsem).wait()
+    pltpu.make_async_copy(att_in, att_in, att_rsem).wait()
+
 
     def project(which):
-        return dot_nt(att_ref[...], wo[pl.ds(pl.multiple_of(which * Q, Q), Q), :])
+        f = pl.ds(pl.multiple_of(which * Q, Q), Q)
+        return dot_nt(att_out[c], wo2[c, f, :]) + dot_nt(att_in[...], wo2[1 - c, f, :])
 
     proj_copies = []
     for i in (1, 0, 2):
@@ -127,7 +337,7 @@
         copy = remote(proj_send.at[i], proj_recv.at[2 - i], proj_ssem.at[i], proj_rsem.at[2 - i], r, peers[i])
         copy.start()
         proj_copies.append(copy)
-    loads[1].wait()
+    loads[0].wait()
     own = res[...].astype(F32) + project(y)
     for i in range(3):
         pltpu.make_async_copy(proj_recv.at[i], proj_recv.at[i], proj_rsem.at[i]).wait()
@@ -141,7 +351,7 @@
         copy = remote(stat_send, stat_recv.at[2 - i], stat_ssem.at[i], stat_rsem.at[2 - i], r, peers[i])
         copy.start()
         stat_copies.append(copy)
-    loads[2].wait()
+    loads[1].wait()
     for i in range(3):
         pltpu.make_async_copy(stat_recv.at[i], stat_recv.at[i], stat_rsem.at[i]).wait()
     squares = stat_send[...] + stat_recv[0] + stat_recv[1] + stat_recv[2]
@@ -218,8 +428,8 @@
         select = jnp.where(line_id == (row_id >> 1) * 8 + 2 * k + (row_id & 1), 1.0, 0.0).astype(BF)
         for q in range(4):
             xbuf[512:640, Q * q + 128 * k:Q * q + 128 * k + 128] = dot(select, rows2[q, :, Q:WIDE]).astype(BF)
+    loads[2].wait()
     loads[3].wait()
-    loads[4].wait()
 
     def inner(n, c):
         cols = pl.ds(pl.multiple_of(n * 256, 256), 256)
@@ -229,7 +439,7 @@
         return c
 
     lax.fori_loop(0, HID // 256, inner, 0)
-    loads[5].wait()
+    loads[4].wait()
 
     line_of = iota((512, 512), 0)
     row_of = iota((512, 512), 1)
@@ -283,25 +493,37 @@
     mixture = dot(g_main[0], back) + dot(g_main[1], back) + dot(g_rem[0], masked) + dot(g_rem[1], masked)
     out_ref[...] = (hid[...] + mixture).astype(BF)
 
-    for copy in proj_copies + stat_copies + ag_copies + rs:
+    for copy in mate_copies + wo_copies + proj_copies + stat_copies + ag_copies + rs:
         copy.wait_send()
+    few = wo.at[0, pl.ds(0, 7)]
+    pltpu.make_async_copy(few, few, wo_ssem.at[0]).wait()
+    pltpu.make_async_copy(wo.at[c], wo.at[c], pair_ssem).wait()
     for sem, ref in ((a2a_ssem, disp), (ret_ssem, fin)):
         view = ref.at[pl.ds(0, NREQ - 1)]
         pltpu.make_async_copy(view, view, sem).wait()
-
-
-def layer_call(att, wo, residual, gain, logits, routes, placement, wg, wu, wd):
+    for s in range(1, 9):
+        for k in range(2):
+            view = kv.at[s, k]
+            pltpu.make_async_copy(view, view, kv_ssem.at[s, k]).wait()
+
+
+def layer_call(*args):
     vmem = pl.BlockSpec(memory_space=pltpu.VMEM)
+    smem = pl.BlockSpec(memory_space=pltpu.SMEM)
     hbm = pl.BlockSpec(memory_space=pl.ANY)
     dma = pltpu.SemaphoreType.DMA
     chunk = (NREQ, 8, WIDE)
     return pl.pallas_call(
         layer_kernel,
         out_shape=jax.ShapeDtypeStruct((TOK, Q), BF),
-        in_specs=[vmem, hbm, hbm, hbm, vmem, vmem, vmem, hbm, hbm, hbm],
+        in_specs=[hbm, hbm, hbm, hbm, smem, hbm, hbm, hbm, vmem, vmem, vmem, hbm, hbm, hbm],
         out_specs=vmem,
         scratch_shapes=[
-            pltpu.VMEM((D, D // 2), BF), pltpu.VMEM((TOK, Q), BF), pltpu.VMEM((1, Q), F32),
+            pltpu.VMEM((9, 2, 2, 512, HEAD_SIZE), BF), pltpu.VMEM((2, 2, 512, HEAD_SIZE), BF),
+            pltpu.VMEM((2, HEAD_SIZE, 1024), BF), pltpu.VMEM((HEAD_SIZE, 512), BF), pltpu.VMEM((2, 1, TOK), jnp.int32),
+            pltpu.VMEM((2, 1, 1024), F32), pltpu.VMEM((2, 1, 1024), F32), pltpu.VMEM((2, HEAD_SIZE, 1024), F32),
+            pltpu.VMEM((2, TOK, 512), BF), pltpu.VMEM((TOK, 512), BF),
+            pltpu.VMEM((2, NREQ, 32, 512), BF), pltpu.VMEM((TOK, Q), BF), pltpu.VMEM((1, Q), F32),
             pltpu.VMEM((D, HID), BF), pltpu.VMEM((D, HID), BF), pltpu.VMEM((D, HID), BF),
             pltpu.VMEM((3, TOK, Q), BF), pltpu.VMEM((3, TOK, Q), BF), pltpu.VMEM((TOK, Q), F32),
             pltpu.VMEM((8, TOK), F32), pltpu.VMEM((3, 8, TOK), F32),
@@ -310,104 +532,25 @@
             pltpu.VMEM(chunk, BF), pltpu.VMEM((4,) + chunk, BF), pltpu.VMEM((640, D), BF), pltpu.VMEM((640, HID), BF),
             pltpu.VMEM((4,) + chunk, BF), pltpu.VMEM((32, 8, WIDE), BF), pltpu.VMEM((32, 8, WIDE), BF),
             pltpu.VMEM(chunk, BF), pltpu.VMEM(chunk, BF), pltpu.VMEM(chunk, BF), pltpu.VMEM(chunk, BF),
-            dma((6,)), dma((3,)), dma((3,)), dma((3,)), dma((3,)),
+            dma((9, 2)), dma((9, 2)), dma((9,)), dma((4,)), dma((5,)), dma((1,)), dma((1,)), dma((7,)), dma((7,)),
+            dma, dma, dma, dma,
+            dma((5,)), dma((3,)), dma((3,)), dma((3,)), dma((3,)),
             dma, dma((8,)), dma((3, 8)), dma((3, 8)), dma((6,)), dma((6,)), dma, dma((8,)), dma,
         ],
         compiler_params=pltpu.CompilerParams(
-            collective_id=1, has_side_effects=True, vmem_limit_bytes=56 << 20
+            collective_id=1, has_side_effects=True, vmem_limit_bytes=60 << 20
         ),
         name="layer",
-    )(att, wo, residual, gain, logits, routes, placement, wg, wu, wd)
-
-
-def shifted(value, axis, steps):
-    count = lax.axis_size(axis)
-    initial, last = (max(0, -steps), min(count, count - steps))
-    return lax.ppermute(value, axis, [(source, source + steps) for source in range(initial, last)])
-
-
-def step_back(keys_in_block, values_in_block):
-    return shifted((keys_in_block, values_in_block), "req", 1)
+    )(*args)
 
 
 def per_device(
     residual, queries, rotated_key_rows, values, req_start, head_sink_logit, out_proj, mid_gain,
     router_logits, routes, placement, w_gate, w_up, w_down,
 ):
-    tok_count = residual.shape[0]
-    req_size = lax.axis_size("req")
-    own_req = lax.axis_index("req")
-    query_group_width = QUERY_HEADS // KEY_VALUE_HEADS
-    kv_heads = rotated_key_rows.shape[1] // HEAD_SIZE
-    shard_queries = queries.reshape(tok_count, kv_heads, query_group_width, HEAD_SIZE)
-    local_keys = rotated_key_rows.reshape(tok_count, kv_heads, HEAD_SIZE)
-    local_values = values.reshape(tok_count, kv_heads, HEAD_SIZE)
-    win_span = min(16, req_size // 2)
-    window = win_span * tok_count
-    query_pos = own_req * tok_count + jnp.arange(tok_count, dtype=jnp.int32)
-    logit_scale_factor = HEAD_SIZE ** (-0.5)
-
-    def attend(carry_state, keys_in_block, values_in_block, key_first):
-        running_max, row_total, weighted_value_sum = carry_state
-        attention_logits = (
-            jnp.einsum(
-                "veck,uek->ecvu", shard_queries, keys_in_block, preferred_element_type=jnp.float32
-            )
-            * logit_scale_factor
-        )
-        key_pos = key_first + jnp.arange(keys_in_block.shape[0], dtype=jnp.int32)
-        visible = (
-            (key_pos[None, :] >= req_start[:, None])
-            & (key_pos[None, :] <= query_pos[:, None])
-            & (query_pos[:, None] - key_pos[None, :] < window)
-        )
-        attention_logits = jnp.where(visible[None, None], attention_logits, -jnp.inf)
-        new_max = jnp.maximum(running_max, jnp.max(attention_logits, axis=-1))
-        probs = jnp.exp(attention_logits - new_max[..., None])
-        factor = jnp.exp(running_max - new_max)
-        row_total = row_total * factor + jnp.sum(probs, axis=-1)
-        weighted_value_sum = weighted_value_sum * factor[..., None] + jnp.einsum(
-            "plyw,wpj->plyj",
-            probs.astype(jnp.bfloat16),
-            values_in_block,
-            preferred_element_type=jnp.float32,
-        )
-        return (new_max, row_total, weighted_value_sum)
-
-    initial_sink_logit = jnp.broadcast_to(
-        head_sink_logit.reshape(kv_heads, query_group_width, 1),
-        (kv_heads, query_group_width, tok_count),
-    )
-    carry_state = (
-        initial_sink_logit,
-        jnp.ones((kv_heads, query_group_width, tok_count), jnp.float32),
-        jnp.zeros((kv_heads, query_group_width, tok_count, HEAD_SIZE), jnp.float32),
-    )
-    carry_state = attend(carry_state, local_keys, local_values, own_req * tok_count)
-
-    def pair_step(step_idx, loop_carry):
-        folded, near_keys, near_values = loop_carry
-        mid_keys, mid_values = step_back(near_keys, near_values)
-        far_keys, far_values = step_back(mid_keys, mid_values)
-        key_first = (own_req - 2 * step_idx - 2) * tok_count
-        folded = attend(
-            folded,
-            jnp.concatenate([far_keys, mid_keys], 0),
-            jnp.concatenate([far_values, mid_values], 0),
-            key_first,
-        )
-        return (folded, far_keys, far_values)
-
-    carry_state, unused_keys, unused_values = lax.fori_loop(
-        0, win_span // 2, pair_step, (carry_state, local_keys, local_values)
-    )
-    running_max, row_total, weighted_value_sum = carry_state
-    attended = (weighted_value_sum / row_total[..., None]).astype(jnp.bfloat16)
-    flat_attended = jnp.transpose(attended, (2, 0, 1, 3)).reshape(tok_count, -1)
-    wo = lax.all_gather(out_proj.T, "req", axis=0, tiled=True)
     return layer_call(
-        flat_attended, wo, residual, mid_gain.reshape(1, D), router_logits.T, routes.T,
-        placement.reshape(1, NREQ), w_gate[0], w_up[0], w_down[0],
+        queries, rotated_key_rows, values, req_start.reshape(1, TOK), head_sink_logit, out_proj.T, residual,
+        mid_gain.reshape(1, D), router_logits.T, routes.T, placement.reshape(1, NREQ), w_gate[0], w_up[0], w_down[0],
     )
 
 

time: 356 us -> 186 us (0.52)
  waiting for transfers between devices: 81.2 us -> 0 us
  starting transfers between devices: 74.9 us -> 0 us
  Pallas kernels: 133 us -> 184 us
  matrix products: 29.1 us -> 0 us
  between operations: 13.5 us -> 0.01 us
  other arithmetic: 10.6 us -> 0 us
  local copies, waits for them, and re-layouts: 10.3 us -> 1.67 us
    ppermute x32 -> x0, waiting for transfers between devices: 80.5 us -> none  [shifted(): lax.ppermute(value, axis, [(source, source + steps) for source in range(i...]
    ppermute x32 -> x0, starting transfers between devices: 74.9 us -> none  [shifted(): lax.ppermute(value, axis, [(source, source + steps) for source in range(i...]
    pallas_call x1, Pallas kernels: 133 us -> 184 us  [layer_call(): pl.pallas_call(layer_kernel, out_shape=jax.ShapeDtypeStruct((TOK, Q), BF)...]
    dot_general x18 -> x0, matrix products: 29.1 us -> none  [the longest x9 15.6 us: attend(): jnp.einsum('veck,uek->ecvu', shard_queries, keys_in_block, preferred_elem...]
    reduce_sum x9 -> x0, other arithmetic: 7.31 us -> none  [attend(): row_total = row_total * factor + jnp.sum(probs, axis=-1)]
    unnamed x9 -> x1, local copies, waits for them, and re-layouts: 7.79 us -> 1.67 us
  transfers between devices with their start and end apart: 33 -> 0, of which waited for: 18 -> 0; matrix products, arithmetic and copies ran while one was open for 14% -> 0% of each run, Pallas kernels for 0% -> 0%
where the time goes in v2:
time: 186 us
  Pallas kernels  184 us (99%)
    pallas_call x1, Pallas kernels, layer_call(): pl.pallas_call(layer_kernel, out_shape=jax.ShapeDtypeStruct((TOK, Q), BF)...  184 us

profile of v2, /device:TPU:33, one launch (start us, length us, event | category | flops | bytes accessed | tf_op | source)
XLA Modules:
  0.0 185.8 jit_solution(5906935063163368025)
XLA Ops:
  0.0 184.2 %layer.1 = bf16[256,512]{1,0:T(8,128)(2,1)} custom-call(bf16[256,1024]{1,0:T(8,128)(2,1)} %q_hbm.1, bf16[256,512]{1,0:T(8,128)(2,1)} %k_hbm.1, bf16[256,512]{1,0:T(8,128)(2,1)} %v_hbm.1, s32[1,256]{1,0:T(1,128)} %bitcast.16, f32[8]{0:T(128)} %sink_ref.1, bf16[32,1024]{1,0:T(8,128)(2,1)} %bitcast.12, bf16[256,2048]{1,0:T(8,128)(2,1)} %res_hbm.1, ...), custom_call_target="tpu_custom_call" | custom-call | tf_op jit(solution)/shard_map/layer/pallas_call | solution.py:516
  184.2 1.7 copy.16

commit v3 on v2

--- a/solution.py
+++ b/solution.py
@@ -33,6 +33,10 @@
     return lax.dot_general(a, b, (((1,), (1,)), ((), ())), preferred_element_type=F32)
 
 
+def dot_tn(a, b):
+    return lax.dot_general(a, b, (((0,), (0,)), ((), ())), preferred_element_type=F32)
+
+
 def iota(shape, dim):
     return lax.broadcasted_iota(jnp.int32, shape, dim)
 
@@ -44,7 +48,7 @@
     )
 
 
-SCALE2 = HEAD_SIZE ** (-0.5) * 1.4426950408889634
+SCALE = HEAD_SIZE ** (-0.5)
 MASKED = -1e30
 
 
@@ -52,7 +56,7 @@
     q_hbm, k_hbm, v_hbm, start_hbm, sink_ref, wo_hbm, res_hbm, gain_hbm, logits_ref, routes_ref, placement_ref,
     wg_hbm, wu_hbm, wd_hbm,
     out_ref,
-    kv, qb, qt, vt, starts, peak, mass, acc, att_out, att_in,
+    kv, qb, qt, starts, peak, mass, acc, att_out, att_in,
     wo, res, gain, wg, wu, wd,
     proj_send, proj_recv, hid, stat_send, stat_recv,
     e_main, e_rem, g_main, g_rem,
@@ -74,13 +78,11 @@
 
     bar = pltpu.get_barrier_semaphore()
 
-    def greet(o, c):
-        pl.semaphore_signal(bar, inc=1, device_id=(lax.rem(r + o, NREQ), y), device_id_type=MESH)
-        return c
-
-    lax.fori_loop(1, NREQ, greet, 0)
-    for p in peers:
-        pl.semaphore_signal(bar, inc=1, device_id=(r, p), device_id_type=MESH)
+    near = [(lax.rem(r + 8, NREQ), y), (lax.rem(r + NREQ - 8, NREQ), y)]
+    near += [(z * 8 + lax.rem(r + k, 8), y) for k in range(1, 8)]
+    near += [(r, p) for p in peers]
+    for device in near:
+        pl.semaphore_signal(bar, inc=1, device_id=device, device_id_type=MESH)
 
     y_cols = pl.ds(pl.multiple_of(y * Q, Q), Q)
     loads = [
@@ -107,7 +109,7 @@
     pltpu.make_async_copy(start_hbm, starts.at[c], loc_sem.at[3]).start()
     pltpu.make_async_copy(wo_hbm.at[:, pl.ds(pl.multiple_of(c * 512, 512), 512)], wo.at[c, r], loc_sem.at[4]).start()
 
-    pl.semaphore_wait(bar, NREQ - 1 + 3)
+    pl.semaphore_wait(bar, len(near))
 
     mate_copies = []
 
@@ -152,7 +154,9 @@
         took(4, k)
         send(4, 8, k, 1, 0)
         for d in (1, 3):
-            send(4, d + 4 * (1 - wraps[d]), k, 0, d)
+            @pl.when(wraps[d] == 1)
+            def _():
+                send(4, d, k, 0, d)
 
     def took8(k):
         took(8, k)
@@ -165,6 +169,12 @@
         took(1, k)
         took(3, k)
         send(1 + 2 * odd, 2, k, 0, 1 + 2 * odd)
+        if k == 1:
+            for d in (1, 3):
+                @pl.when(wraps[d] == 0)
+                def _():
+                    send(4, d + 4, 0, 0, d)
+                    send(4, d + 4, 1, 0, d)
 
     def took2(k):
         took(2, k)
@@ -184,22 +194,23 @@
             else:
                 give()
 
-    def ring(t):
-        g = pl.ds(lax.rem(z + t, NZ) * 8, 8)
-        view = wo.at[c, g]
-        if t == 0:
+    def ring(t, half):
+        view = wo.at[c, pl.ds(lax.rem(z + t, NZ) * 8 + 4 * half, 4)]
+        if t > 0:
+            pltpu.make_async_copy(view, view, ring_rsem.at[t - 1, half]).wait()
+        elif half == 0:
             few = wo.at[c, pl.ds(z * 8, 7)]
             pltpu.make_async_copy(few, few, wo_rsem.at[0]).wait()
             one = wo.at[c, r]
             pltpu.make_async_copy(one, one, loc_sem.at[4]).wait()
-        else:
-            pltpu.make_async_copy(view, view, ring_rsem.at[t - 1]).wait()
         if t < NZ - 1:
-            copy = remote(view, view, ring_ssem.at[t], ring_rsem.at[t], chip_at(NZ - 1, 0), y)
+            copy = remote(view, view, ring_ssem.at[t, half], ring_rsem.at[t, half], chip_at(NZ - 1, 0), y)
             copy.start()
             wo_copies.append(copy)
         remote(view, view, pair_ssem, pair_rsem, mate, y).start()
 
+    ring(0, 0)
+    ring(0, 1)
     view = qb.at[:, :, own_tok]
     pltpu.make_async_copy(view, view, loc_sem.at[2]).wait()
     view = qb.at[:, :, mate_tok]
@@ -212,60 +223,32 @@
     acc[...] = jnp.zeros_like(acc)
     pltpu.make_async_copy(starts.at[c], starts.at[c], loc_sem.at[3]).wait()
     pltpu.make_async_copy(starts.at[1 - c], starts.at[1 - c], half_rsem.at[3]).wait()
-    ring(0)
 
     def attend(s, k):
-        vt[...] = kv[s, k, 1].T
         first = (chip - s) * 512
-
-        def tiles(h, carry):
-            for half in range(2):
-                cols = pl.ds(pl.multiple_of(h * 512 + half * 256, 256), 256)
-                scores = dot(kv[s, k, 0], qt[k, :, cols])
-                at = iota((1, 256), 1) + 256 * half
-                low = jnp.maximum(starts[half] - first, at + (512 * s - 4095))
-                key = iota((512, 256), 0)
-                seen = key >= low
-                if s == 0:
-                    seen = seen & (key <= at)
-                scores = jnp.where(seen, scores, MASKED)
-                old = peak[k, :, cols]
-                new = jnp.maximum(old, jnp.max(scores, axis=0, keepdims=True))
-                probs = jnp.exp2((scores - new) * SCALE2)
-                alpha = jnp.exp2((old - new) * SCALE2)
-                peak[k, :, cols] = new
-                mass[k, :, cols] = mass[k, :, cols] * alpha + jnp.sum(probs, axis=0, keepdims=True)
-                acc[k, :, cols] = acc[k, :, cols] * alpha + dot(vt[...], probs.astype(BF))
-            return carry
-
-        lax.fori_loop(0, 2, tiles, 0)
+        scores = dot(kv[s, k, 0], qt[k])
+        token = iota((1, 1024), 1) & 511
+        both = jnp.concatenate([starts[0], starts[1]], axis=1)
+        low = jnp.maximum(jnp.concatenate([both, both], axis=1) - first, token + (512 * s - 4095))
+        key = iota((512, 1024), 0)
+        seen = key >= low
+        if s == 0:
+            seen = seen & (key <= token)
+        scores = jnp.where(seen, scores, MASKED)
+        old = peak[k]
+        new = jnp.maximum(old, jnp.max(scores, axis=0, keepdims=True))
+        probs = jnp.exp((scores - new) * SCALE)
+        alpha = jnp.exp((old - new) * SCALE)
+        peak[k] = new
+        mass[k] = mass[k] * alpha + jnp.sum(probs, axis=0, keepdims=True)
+        acc[k] = acc[k] * alpha + dot_tn(kv[s, k, 1], probs.astype(BF))
 
     attend(0, 0)
+    attend(0, 1)
     took4(0)
-    attend(0, 1)
-    took13(0)
-    ring(1)
+    ring(1, 0)
     attend(4, 0)
-    took4(1)
-    attend(1, 0)
-    took13(1)
-    attend(3, 0)
-    ring(2)
-    attend(4, 1)
-    attend(1, 1)
-    took8(0)
-    attend(3, 1)
-    took2(0)
-    ring(3)
-    attend(8, 0)
-    took8(1)
-    attend(2, 0)
-    took2(1)
-    attend(8, 1)
-    ring(4)
-    attend(2, 1)
-    took(5, 0)
-    attend(5, 0)
+    ring(1, 1)
     route0, route1 = routes_ref[0:1, :], routes_ref[1:2, :]
     dest = iota((NREQ, TOK), 0)
     hot0 = jnp.where(dest == route0, 1.0, 0.0)
@@ -299,18 +282,45 @@
         ref[1] = (gate - high.astype(F32)).astype(BF)
 
 
+    took13(0)
+    took4(1)
+    ring(2, 0)
+    attend(1, 0)
+    attend(3, 0)
+    ring(2, 1)
+    attend(4, 1)
+    took13(1)
+    took8(0)
+    ring(3, 0)
+    attend(1, 1)
+    attend(3, 1)
+    ring(3, 1)
+    took2(0)
+    attend(8, 0)
+    ring(4, 0)
+    took8(1)
+    attend(2, 0)
+    ring(4, 1)
+    took2(1)
+    attend(8, 1)
+    ring(5, 0)
+    attend(2, 1)
+    ring(5, 1)
+    took(5, 0)
+    attend(5, 0)
+    ring(6, 0)
     took(7, 0)
     attend(7, 0)
-    ring(5)
+    ring(6, 1)
     took(5, 1)
     attend(5, 1)
+    ring(7, 0)
     took(7, 1)
     attend(7, 1)
-    ring(6)
+    ring(7, 1)
     for k in range(2):
         took(6, k)
         attend(6, k)
-    ring(7)
 
     for k in range(2):
         out = acc[k] / mass[k]
@@ -520,7 +530,7 @@
         out_specs=vmem,
         scratch_shapes=[
             pltpu.VMEM((9, 2, 2, 512, HEAD_SIZE), BF), pltpu.VMEM((2, 2, 512, HEAD_SIZE), BF),
-            pltpu.VMEM((2, HEAD_SIZE, 1024), BF), pltpu.VMEM((HEAD_SIZE, 512), BF), pltpu.VMEM((2, 1, TOK), jnp.int32),
+            pltpu.VMEM((2, HEAD_SIZE, 1024), BF), pltpu.VMEM((2, 1, TOK), jnp.int32),
             pltpu.VMEM((2, 1, 1024), F32), pltpu.VMEM((2, 1, 1024), F32), pltpu.VMEM((2, HEAD_SIZE, 1024), F32),
             pltpu.VMEM((2, TOK, 512), BF), pltpu.VMEM((TOK, 512), BF),
             pltpu.VMEM((2, NREQ, 32, 512), BF), pltpu.VMEM((TOK, Q), BF), pltpu.VMEM((1, Q), F32),
@@ -532,7 +542,7 @@
             pltpu.VMEM(chunk, BF), pltpu.VMEM((4,) + chunk, BF), pltpu.VMEM((640, D), BF), pltpu.VMEM((640, HID), BF),
             pltpu.VMEM((4,) + chunk, BF), pltpu.VMEM((32, 8, WIDE), BF), pltpu.VMEM((32, 8, WIDE), BF),
             pltpu.VMEM(chunk, BF), pltpu.VMEM(chunk, BF), pltpu.VMEM(chunk, BF), pltpu.VMEM(chunk, BF),
-            dma((9, 2)), dma((9, 2)), dma((9,)), dma((4,)), dma((5,)), dma((1,)), dma((1,)), dma((7,)), dma((7,)),
+            dma((9, 2)), dma((9, 2)), dma((9,)), dma((4,)), dma((5,)), dma((1,)), dma((1,)), dma((7, 2)), dma((7, 2)),
             dma, dma, dma, dma,
             dma((5,)), dma((3,)), dma((3,)), dma((3,)), dma((3,)),
             dma, dma((8,)), dma((3, 8)), dma((3, 8)), dma((6,)), dma((6,)), dma, dma((8,)), dma,

time: 186 us -> 179 us (0.962)
  Pallas kernels: 184 us -> 177 us
    pallas_call x1, Pallas kernels: 184 us -> 177 us  [layer_call(): pl.pallas_call(layer_kernel, out_shape=jax.ShapeDtypeStruct((TOK, Q), BF)...]
where the time goes in v3:
time: 179 us
  Pallas kernels  177 us (99%)
    pallas_call x1, Pallas kernels, layer_call(): pl.pallas_call(layer_kernel, out_shape=jax.ShapeDtypeStruct((TOK, Q), BF)...  177 us

profile of v3, /device:TPU:33, one launch (start us, length us, event | category | flops | bytes accessed | tf_op | source)
XLA Modules:
  0.0 178.9 jit_solution(17063548511259341154)
XLA Ops:
  0.0 177.2 %layer.1 = bf16[256,512]{1,0:T(8,128)(2,1)} custom-call(bf16[256,1024]{1,0:T(8,128)(2,1)} %q_hbm.1, bf16[256,512]{1,0:T(8,128)(2,1)} %k_hbm.1, bf16[256,512]{1,0:T(8,128)(2,1)} %v_hbm.1, s32[1,256]{1,0:T(1,128)} %bitcast.16, f32[8]{0:T(128)} %sink_ref.1, bf16[32,1024]{1,0:T(8,128)(2,1)} %bitcast.12, bf16[256,2048]{1,0:T(8,128)(2,1)} %res_hbm.1, ...), custom_call_target="tpu_custom_call" | custom-call | tf_op jit(solution)/shard_map/layer/pallas_call | solution.py:526
  177.2 1.7 copy.16

commit v4 on v3

--- a/solution.py
+++ b/solution.py
@@ -379,16 +379,21 @@
 
     disp2[:, Q:WIDE] = by_piece([spread[:, 128 * k:128 * k + 128] for k in range(4)]).astype(BF)
 
-    def exchange(source, target, send_sem, recv_sems):
-        for dz in Z_ORDER:
-            def push(k, c):
-                d = lax.rem(z + dz, NZ) * 8 + lax.rem(r + k, 8)
-                remote(source.at[d], target.at[r], send_sem, recv_sems.at[z], d, y).start()
-                return c
-            lax.fori_loop(1 if dz == 0 else 0, 8, push, 0)
-        copy = pltpu.make_async_copy(source.at[r], target.at[r], own_sem)
-        copy.start()
-        copy.wait()
+    def exchange(source, target, send_sem, recv_sems, picks, ordered):
+        for i in picks:
+            g = lax.rem(z + Z_ORDER[i], NZ)
+            base = i * 8 if ordered else g * 8
+
+            def push(k, carry):
+                m = lax.rem(r + k, 8)
+                remote(source.at[base + m], target.at[r], send_sem, recv_sems.at[z], g * 8 + m, y).start()
+                return carry
+
+            lax.fori_loop(1 if i == 0 else 0, 8, push, 0)
+            if i == 0:
+                copy = pltpu.make_async_copy(source.at[base + lax.rem(r, 8)], target.at[r], own_sem)
+                copy.start()
+                copy.wait()
 
     def arrived(target, recv_sems, dz):
         g = lax.rem(z + dz, NZ)
@@ -397,7 +402,7 @@
         pltpu.make_async_copy(view, view, recv_sems.at[g]).wait()
 
     mine = rows.at[y]
-    exchange(disp, mine, a2a_ssem, a2a_rsem)
+    exchange(disp, mine, a2a_ssem, a2a_rsem, range(8), False)
 
     ag_copies = []
 
@@ -420,8 +425,8 @@
             ag_copies.append(copy)
         if i > 0:
             forward(i - 1)
-    forward(7)
-    for i in range(8):
+
+    def gathered(i):
         g = pl.ds(lax.rem(z + Z_ORDER[i], NZ) * 8, 8)
         here, side = (yp, 1) if i % 2 == 0 else (ym, 0)
         view = rows.at[here, g]
@@ -430,70 +435,93 @@
         pltpu.make_async_copy(view, view, ag_rsem.at[2, i]).wait()
 
     rows2 = rows.reshape(4, 512, WIDE)
-    row_id = iota((128, 512), 0)
-    line_id = iota((128, 512), 1)
-    for q in range(4):
-        xbuf[0:512, Q * q:Q * q + Q] = rows2[q, :, 0:Q]
-    for k in range(4):
-        select = jnp.where(line_id == (row_id >> 1) * 8 + 2 * k + (row_id & 1), 1.0, 0.0).astype(BF)
+    part2 = part.reshape(4, 512, WIDE)
+    fin2 = fin.reshape(512, WIDE)
+    from_l2, from_r2 = from_l.reshape(512, WIDE), from_r.reshape(512, WIDE)
+    hop_l2, hop_r2 = hop_l.reshape(2, 128, WIDE), hop_r.reshape(2, 128, WIDE)
+    row_id, line_id = iota((64, 256), 0), iota((64, 256), 1)
+    line_of, row_of = iota((256, 256), 0), iota((256, 256), 1)
+    scatter = jnp.where(
+        line_of == ((row_of & 63) >> 1) * 8 + 2 * (row_of >> 6) + (row_of & 1), 1.0, 0.0
+    ).astype(BF)
+    rs = []
+
+    def hidden_units(p):
+        starts_at = [pl.multiple_of(lax.rem(z + Z_ORDER[4 * p + j], NZ) * 64, 64) for j in range(4)]
         for q in range(4):
-            xbuf[512:640, Q * q + 128 * k:Q * q + 128 * k + 128] = dot(select, rows2[q, :, Q:WIDE]).astype(BF)
+            for j in range(4):
+                xbuf[64 * j:64 * j + 64, Q * q:Q * q + Q] = rows2[q, pl.ds(starts_at[j], 64), 0:Q]
+            tails = jnp.concatenate([rows2[q, pl.ds(at, 64), Q:WIDE] for at in starts_at], axis=0)
+            for k in range(4):
+                select = jnp.where(line_id == (row_id >> 1) * 8 + 2 * k + (row_id & 1), 1.0, 0.0).astype(BF)
+                xbuf[256:320, Q * q + 128 * k:Q * q + 128 * k + 128] = dot(select, tails).astype(BF)
+
+        def inner(n, carry):
+            cols = pl.ds(pl.multiple_of(n * 256, 256), 256)
+            gate = dot(xbuf[...], wg[:, cols])
+            up = dot(xbuf[...], wu[:, cols])
+            act[:, cols] = (gate / (1.0 + jnp.exp(-gate)) * up).astype(BF)
+            return carry
+
+        lax.fori_loop(0, HID // 256, inner, 0)
+
+    def reduce_send(p, n, src, dst, device):
+        copy = remote(src, dst, rs_ssem.at[p, n], rs_rsem.at[p, n], r, device)
+        copy.start()
+        rs.append(copy)
+
+    def outputs(p):
+        low, high = pl.ds(32 * p, 16), pl.ds(32 * p + 16, 16)
+        for j, which in enumerate((y2, yp, ym, y)):
+            piece_out = dot_nt(act[...], wd[pl.ds(pl.multiple_of(which * Q, Q), Q), :])
+            part2[j, 256 * p:256 * p + 256, 0:Q] = piece_out[0:256].astype(BF)
+            tail = piece_out[256:320].astype(BF)
+            stacked = jnp.concatenate([tail[:, 128 * k:128 * k + 128] for k in range(4)], axis=0)
+            part2[j, 256 * p:256 * p + 256, Q:WIDE] = dot(scatter, stacked).astype(BF)
+            if j == 0:
+                reduce_send(p, 0, part.at[0, low], hop_l.at[p], yp)
+                reduce_send(p, 1, part.at[0, high], hop_r.at[p], ym)
+            if j == 1:
+                reduce_send(p, 2, part.at[1, high], from_l.at[high], yp)
+            if j == 2:
+                reduce_send(p, 3, part.at[2, low], from_r.at[low], ym)
+
+    def hop(p):
+        low, high = pl.ds(32 * p, 16), pl.ds(32 * p + 16, 16)
+        low2, high2 = slice(256 * p, 256 * p + 128), slice(256 * p + 128, 256 * p + 256)
+        pltpu.make_async_copy(hop_l.at[p], hop_l.at[p], rs_rsem.at[p, 0]).wait()
+        part2[1, low2, :] = (part2[1, low2, :].astype(F32) + hop_l2[p].astype(F32)).astype(BF)
+        reduce_send(p, 4, part.at[1, low], from_l.at[low], yp)
+        pltpu.make_async_copy(hop_r.at[p], hop_r.at[p], rs_rsem.at[p, 1]).wait()
+        part2[2, high2, :] = (part2[2, high2, :].astype(F32) + hop_r2[p].astype(F32)).astype(BF)
+        reduce_send(p, 5, part.at[2, high], from_r.at[high], ym)
+
+    def give_back(p):
+        low, high = pl.ds(32 * p, 16), pl.ds(32 * p + 16, 16)
+        for ref, half, k in ((from_l, high, 2), (from_r, low, 3), (from_l, low, 4), (from_r, high, 5)):
+            view = ref.at[half]
+            pltpu.make_async_copy(view, view, rs_rsem.at[p, k]).wait()
+        at = slice(256 * p, 256 * p + 256)
+        total_out = part2[3, at, :].astype(F32) + from_l2[at, :].astype(F32) + from_r2[at, :].astype(F32)
+        fin2[at, :] = total_out.astype(BF)
+        exchange(fin, ret, ret_ssem, ret_rsem, range(4 * p, 4 * p + 4), True)
+
+    for i in range(4):
+        gathered(i)
     loads[2].wait()
     loads[3].wait()
-
-    def inner(n, c):
-        cols = pl.ds(pl.multiple_of(n * 256, 256), 256)
-        gate = dot(xbuf[...], wg[:, cols])
-        up = dot(xbuf[...], wu[:, cols])
-        act[:, cols] = (gate / (1.0 + jnp.exp(-gate)) * up).astype(BF)
-        return c
-
-    lax.fori_loop(0, HID // 256, inner, 0)
+    hidden_units(0)
+    forward(7)
     loads[4].wait()
-
-    line_of = iota((512, 512), 0)
-    row_of = iota((512, 512), 1)
-    scatter = jnp.where(
-        line_of == ((row_of & 127) >> 1) * 8 + 2 * (row_of >> 7) + (row_of & 1), 1.0, 0.0
-    ).astype(BF)
-    part2 = part.reshape(4, 512, WIDE)
-    for j, which in enumerate((y2, yp, ym, y)):
-        piece_out = dot_nt(act[...], wd[pl.ds(pl.multiple_of(which * Q, Q), Q), :])
-        part2[j, :, 0:Q] = piece_out[0:512].astype(BF)
-        tail = piece_out[512:640].astype(BF)
-        stacked = jnp.concatenate([tail[:, 128 * k:128 * k + 128] for k in range(4)], axis=0)
-        part2[j, :, Q:WIDE] = dot(scatter, stacked).astype(BF)
-        if j == 0:
-            rs = [
-                remote(part.at[0, pl.ds(0, 32)], hop_l, rs_ssem.at[0], rs_rsem.at[0], r, yp),
-                remote(part.at[0, pl.ds(32, 32)], hop_r, rs_ssem.at[1], rs_rsem.at[1], r, ym),
-            ]
-            rs[0].start()
-            rs[1].start()
-        if j == 1:
-            rs.append(remote(part.at[1, pl.ds(32, 32)], from_l.at[pl.ds(32, 32)], rs_ssem.at[2], rs_rsem.at[2], r, yp))
-            rs[2].start()
-        if j == 2:
-            rs.append(remote(part.at[2, pl.ds(0, 32)], from_r.at[pl.ds(0, 32)], rs_ssem.at[3], rs_rsem.at[3], r, ym))
-            rs[3].start()
-    hop_l2, hop_r2 = hop_l.reshape(256, WIDE), hop_r.reshape(256, WIDE)
-    pltpu.make_async_copy(hop_l, hop_l, rs_rsem.at[0]).wait()
-    part2[1, 0:256, :] = (part2[1, 0:256, :].astype(F32) + hop_l2[...].astype(F32)).astype(BF)
-    rs.append(remote(part.at[1, pl.ds(0, 32)], from_l.at[pl.ds(0, 32)], rs_ssem.at[4], rs_rsem.at[4], r, yp))
-    rs[4].start()
-    pltpu.make_async_copy(hop_r, hop_r, rs_rsem.at[1]).wait()
-    part2[2, 256:512, :] = (part2[2, 256:512, :].astype(F32) + hop_r2[...].astype(F32)).astype(BF)
-    rs.append(remote(part.at[2, pl.ds(32, 32)], from_r.at[pl.ds(32, 32)], rs_ssem.at[5], rs_rsem.at[5], r, ym))
-    rs[5].start()
-    low, high = pl.ds(0, 32), pl.ds(32, 32)
-    for ref, half, k in ((from_l, high, 2), (from_r, low, 3), (from_l, low, 4), (from_r, high, 5)):
-        view = ref.at[half]
-        pltpu.make_async_copy(view, view, rs_rsem.at[k]).wait()
-    fin2 = fin.reshape(512, WIDE)
-    from_l2, from_r2 = from_l.reshape(512, WIDE), from_r.reshape(512, WIDE)
-    fin2[...] = (part2[3].astype(F32) + from_l2[...].astype(F32) + from_r2[...].astype(F32)).astype(BF)
-
-    exchange(fin, ret, ret_ssem, ret_rsem)
+    outputs(0)
+    for i in range(4, 8):
+        gathered(i)
+    hidden_units(1)
+    hop(0)
+    outputs(1)
+    give_back(0)
+    hop(1)
+    give_back(1)
     for dz in Z_ORDER:
         arrived(ret, ret_rsem, dz)
     ret2 = ret.reshape(512, WIDE)
@@ -539,13 +567,13 @@
             pltpu.VMEM((8, TOK), F32), pltpu.VMEM((3, 8, TOK), F32),
             pltpu.VMEM((512, TOK), BF), pltpu.VMEM((512, TOK), BF),
             pltpu.VMEM((2, TOK, 512), BF), pltpu.VMEM((2, TOK, 512), BF),
-            pltpu.VMEM(chunk, BF), pltpu.VMEM((4,) + chunk, BF), pltpu.VMEM((640, D), BF), pltpu.VMEM((640, HID), BF),
-            pltpu.VMEM((4,) + chunk, BF), pltpu.VMEM((32, 8, WIDE), BF), pltpu.VMEM((32, 8, WIDE), BF),
+            pltpu.VMEM(chunk, BF), pltpu.VMEM((4,) + chunk, BF), pltpu.VMEM((320, D), BF), pltpu.VMEM((320, HID), BF),
+            pltpu.VMEM((4,) + chunk, BF), pltpu.VMEM((2, 16, 8, WIDE), BF), pltpu.VMEM((2, 16, 8, WIDE), BF),
             pltpu.VMEM(chunk, BF), pltpu.VMEM(chunk, BF), pltpu.VMEM(chunk, BF), pltpu.VMEM(chunk, BF),
             dma((9, 2)), dma((9, 2)), dma((9,)), dma((4,)), dma((5,)), dma((1,)), dma((1,)), dma((7, 2)), dma((7, 2)),
             dma, dma, dma, dma,
             dma((5,)), dma((3,)), dma((3,)), dma((3,)), dma((3,)),
-            dma, dma((8,)), dma((3, 8)), dma((3, 8)), dma((6,)), dma((6,)), dma, dma((8,)), dma,
+            dma, dma((8,)), dma((3, 8)), dma((3, 8)), dma((2, 6)), dma((2, 6)), dma, dma((8,)), dma,
         ],
         compiler_params=pltpu.CompilerParams(
             collective_id=1, has_side_effects=True, vmem_limit_bytes=60 << 20

time: 179 us -> 168 us (0.939)
  Pallas kernels: 177 us -> 167 us
    pallas_call x1, Pallas kernels: 177 us -> 167 us  [layer_call(): pl.pallas_call(layer_kernel, out_shape=jax.ShapeDtypeStruct((TOK, Q), BF)...]
where the time goes in v4:
time: 168 us
  Pallas kernels  167 us (99%)
    pallas_call x1, Pallas kernels, layer_call(): pl.pallas_call(layer_kernel, out_shape=jax.ShapeDtypeStruct((TOK, Q), BF)...  167 us

profile of v4, /device:TPU:33, one launch (start us, length us, event | category | flops | bytes accessed | tf_op | source)
XLA Modules:
  0.0 168.3 jit_solution(4531494974298810278)
XLA Ops:
  0.0 166.7 %layer.1 = bf16[256,512]{1,0:T(8,128)(2,1)} custom-call(bf16[256,1024]{1,0:T(8,128)(2,1)} %q_hbm.1, bf16[256,512]{1,0:T(8,128)(2,1)} %k_hbm.1, bf16[256,512]{1,0:T(8,128)(2,1)} %v_hbm.1, s32[1,256]{1,0:T(1,128)} %bitcast.16, f32[8]{0:T(128)} %sink_ref.1, bf16[32,1024]{1,0:T(8,128)(2,1)} %bitcast.12, bf16[256,2048]{1,0:T(8,128)(2,1)} %res_hbm.1, ...), custom_call_target="tpu_custom_call" | custom-call | tf_op jit(solution)/shard_map/layer/pallas_call | solution.py:554
  166.7 1.7 copy.16

commit v5 on v4

--- a/solution.py
+++ b/solution.py
@@ -23,6 +23,18 @@
 HID = 768
 WIDE = Q + 128
 Z_ORDER = (0, 1, 7, 2, 6, 3, 5, 4)
+PLAN = (
+    ("w0a", 1, 0), ("R", 0, 0), ("w0a", 3, 0), ("w0a", 3, 1), ("z4", 0), ("R", 1, 0), ("heads",), ("R", 0, 1),
+    ("z4", 1), ("w0a", 1, 1), ("w1a", 3, 0), ("w1a", 1, 0), ("w0b", 1, 0), ("R", 2, 0), ("R", 1, 1),
+    ("w1a", 3, 1), ("f", 0), ("w1a", 1, 1), ("z8", 0), ("A", 1, 0), ("w0b", 3, 0), ("R", 2, 1), ("tables",),
+    ("A", 4, 1), ("z8", 1), ("R", 3, 0), ("R", 3, 1), ("A", 0, 1), ("f", 1), ("w1b", 1, 0), ("A", 8, 0),
+    ("A", 1, 1), ("R", 4, 0), ("R", 4, 1), ("A", 3, 0), ("w0b", 1, 1), ("z6", 0), ("A", 3, 1), ("w1b", 1, 1),
+    ("w1b", 3, 1), ("A", 0, 0), ("R", 5, 0), ("A", 2, 0), ("w1b", 3, 0), ("w0b", 3, 1), ("A", 2, 1),
+    ("R", 5, 1), ("z6", 1), ("A", 4, 0), ("A", 5, 0), ("R", 6, 0), ("A", 5, 1), ("A", 6, 0), ("R", 6, 1),
+    ("A", 8, 1), ("A", 6, 1), ("A", 7, 1), ("A", 7, 0), ("R", 7, 0), ("R", 7, 1),
+)
+ALL = (0, 1, 2, 3)
+WRAPS = {1: (3,), 3: (1, 2, 3)}
 
 
 def dot(a, b):
@@ -136,49 +148,32 @@
         view = kv.at[slot, k]
         pltpu.make_async_copy(view, view, kv_rsem.at[slot, k]).wait()
 
-    wraps = {1: (x + 1) // 4, 3: (x + 3) // 4}
-    odd = lax.rem(x, 2)
-
     for k in range(2):
         view = kv.at[0, k, :, own_tok]
         pltpu.make_async_copy(view, view, loc_sem.at[k]).wait()
         view = kv.at[0, k, :, mate_tok]
         pltpu.make_async_copy(view, view, half_rsem.at[k]).wait()
-        send(0, 4, k, 1, 0)
-        for d in (1, 3):
-            @pl.when(wraps[d] == 0)
-            def _():
-                send(0, d, k, 0, d)
-
-    def took4(k):
-        took(4, k)
-        send(4, 8, k, 1, 0)
-        for d in (1, 3):
-            @pl.when(wraps[d] == 1)
-            def _():
-                send(4, d, k, 0, d)
-
-    def took8(k):
-        took(8, k)
-        for d in (1, 3):
-            @pl.when(wraps[d] == 1)
-            def _():
-                send(8, d + 4, k, 0, d)
-
-    def took13(k):
-        took(1, k)
-        took(3, k)
-        send(1 + 2 * odd, 2, k, 0, 1 + 2 * odd)
-        if k == 1:
-            for d in (1, 3):
-                @pl.when(wraps[d] == 0)
-                def _():
-                    send(4, d + 4, 0, 0, d)
-                    send(4, d + 4, 1, 0, d)
-
-    def took2(k):
-        took(2, k)
-        send(2, 6, k, 1, 0)
+
+    def only(columns, action):
+        if len(columns) == 4:
+            action()
+        elif columns:
+            hit = x == columns[0]
+            for v in columns[1:]:
+                hit = hit | (x == v)
+            pl.when(hit)(action)
+
+    waited = {(0, 0): set(ALL), (0, 1): set(ALL)}
+
+    def need(slot, k, columns=ALL):
+        done = waited.setdefault((slot, k), set())
+        left = tuple(v for v in columns if v not in done)
+        done.update(left)
+        only(left, lambda: took(slot, k))
+
+    def along_x(slot, dst, k, d, columns):
+        need(slot, k, columns)
+        only(columns, lambda: send(slot, dst, k, 0, d))
 
     wo_copies = []
     for h in range(2):
@@ -209,20 +204,19 @@
             wo_copies.append(copy)
         remote(view, view, pair_ssem, pair_rsem, mate, y).start()
 
-    ring(0, 0)
-    ring(0, 1)
-    view = qb.at[:, :, own_tok]
-    pltpu.make_async_copy(view, view, loc_sem.at[2]).wait()
-    view = qb.at[:, :, mate_tok]
-    pltpu.make_async_copy(view, view, half_rsem.at[2]).wait()
-    for k in range(2):
-        qt[k] = jnp.concatenate([qb[k, 0].T, qb[k, 1].T], axis=1)
-        for h in range(2):
-            peak[k, :, 512 * h:512 * h + 512] = jnp.full((1, 512), sink_ref[4 * c + 2 * k + h] * HEAD_SIZE ** 0.5, F32)
-    mass[...] = jnp.ones_like(mass)
-    acc[...] = jnp.zeros_like(acc)
-    pltpu.make_async_copy(starts.at[c], starts.at[c], loc_sem.at[3]).wait()
-    pltpu.make_async_copy(starts.at[1 - c], starts.at[1 - c], half_rsem.at[3]).wait()
+    def heads():
+        view = qb.at[:, :, own_tok]
+        pltpu.make_async_copy(view, view, loc_sem.at[2]).wait()
+        view = qb.at[:, :, mate_tok]
+        pltpu.make_async_copy(view, view, half_rsem.at[2]).wait()
+        for k in range(2):
+            qt[k] = jnp.concatenate([qb[k, 0].T, qb[k, 1].T], axis=1)
+            for h in range(2):
+                peak[k, :, 512 * h:512 * h + 512] = jnp.full((1, 512), sink_ref[4 * c + 2 * k + h] * HEAD_SIZE ** 0.5, F32)
+        mass[...] = jnp.ones_like(mass)
+        acc[...] = jnp.zeros_like(acc)
+        pltpu.make_async_copy(starts.at[c], starts.at[c], loc_sem.at[3]).wait()
+        pltpu.make_async_copy(starts.at[1 - c], starts.at[1 - c], half_rsem.at[3]).wait()
 
     def attend(s, k):
         first = (chip - s) * 512
@@ -243,84 +237,65 @@
         mass[k] = mass[k] * alpha + jnp.sum(probs, axis=0, keepdims=True)
         acc[k] = acc[k] * alpha + dot_tn(kv[s, k, 1], probs.astype(BF))
 
-    attend(0, 0)
-    attend(0, 1)
-    took4(0)
-    ring(1, 0)
-    attend(4, 0)
-    ring(1, 1)
-    route0, route1 = routes_ref[0:1, :], routes_ref[1:2, :]
-    dest = iota((NREQ, TOK), 0)
-    hot0 = jnp.where(dest == route0, 1.0, 0.0)
-    hot1 = jnp.where(dest == route1, 1.0, 0.0)
-    before = jnp.where(iota((TOK, TOK), 0) < iota((TOK, TOK), 1), 1.0, 0.0).astype(BF)
-    earlier = dot((hot0 + hot1).astype(BF), before)
-    slot0 = route0.astype(F32) * 16.0 + jnp.sum(hot0 * earlier, axis=0, keepdims=True)
-    slot1 = route1.astype(F32) * 16.0 + jnp.sum(hot1 * (earlier + hot0), axis=0, keepdims=True)
-    line = iota((512, TOK), 0)
-    main_id = ((line >> 3) * 16 + (line & 7)).astype(F32)
-    rem_id = ((line >> 3) * 16 + 8 + (line & 1)).astype(F32)
-    e_main[...] = jnp.where((main_id == slot0) | (main_id == slot1), 1.0, 0.0).astype(BF)
-    e_rem[...] = jnp.where((rem_id == slot0) | (rem_id == slot1), 1.0, 0.0).astype(BF)
-    hosts = jnp.where(iota((EXPERTS, NREQ), 0) == placement_ref[...], 1.0, 0.0).astype(BF)
-    logits = logits_ref[...]
-    pick0 = jnp.sum(logits * dot(hosts, hot0.astype(BF)), axis=0, keepdims=True)
-    pick1 = jnp.sum(logits * dot(hosts, hot1.astype(BF)), axis=0, keepdims=True)
-    top = jnp.maximum(pick0, pick1)
-    exp0, exp1 = jnp.exp(pick0 - top), jnp.exp(pick1 - top)
-    total = exp0 + exp1
-    sub = iota((128, TOK), 0)
-    packed = jnp.where(sub == 0, slot0, jnp.where(sub == 1, slot1, jnp.where(sub == 2, exp0 / total, exp1 / total)))
-    turned = packed.T
-    s0, s1, w0, w1 = turned[:, 0:1], turned[:, 1:2], turned[:, 2:3], turned[:, 3:4]
-    col = iota((TOK, 512), 1)
-    for ids, ref in (((col >> 3) * 16 + (col & 7), g_main), ((col >> 3) * 16 + 8 + (col & 1), g_rem)):
-        ids = ids.astype(F32)
-        gate = jnp.where(ids == s0, w0, 0.0) + jnp.where(ids == s1, w1, 0.0)
-        high = gate.astype(BF)
-        ref[0] = high
-        ref[1] = (gate - high.astype(F32)).astype(BF)
-
-
-    took13(0)
-    took4(1)
-    ring(2, 0)
-    attend(1, 0)
-    attend(3, 0)
-    ring(2, 1)
-    attend(4, 1)
-    took13(1)
-    took8(0)
-    ring(3, 0)
-    attend(1, 1)
-    attend(3, 1)
-    ring(3, 1)
-    took2(0)
-    attend(8, 0)
-    ring(4, 0)
-    took8(1)
-    attend(2, 0)
-    ring(4, 1)
-    took2(1)
-    attend(8, 1)
-    ring(5, 0)
-    attend(2, 1)
-    ring(5, 1)
-    took(5, 0)
-    attend(5, 0)
-    ring(6, 0)
-    took(7, 0)
-    attend(7, 0)
-    ring(6, 1)
-    took(5, 1)
-    attend(5, 1)
-    ring(7, 0)
-    took(7, 1)
-    attend(7, 1)
-    ring(7, 1)
-    for k in range(2):
-        took(6, k)
-        attend(6, k)
+    def tables():
+        route0, route1 = routes_ref[0:1, :], routes_ref[1:2, :]
+        dest = iota((NREQ, TOK), 0)
+        hot0 = jnp.where(dest == route0, 1.0, 0.0)
+        hot1 = jnp.where(dest == route1, 1.0, 0.0)
+        before = jnp.where(iota((TOK, TOK), 0) < iota((TOK, TOK), 1), 1.0, 0.0).astype(BF)
+        earlier = dot((hot0 + hot1).astype(BF), before)
+        slot0 = route0.astype(F32) * 16.0 + jnp.sum(hot0 * earlier, axis=0, keepdims=True)
+        slot1 = route1.astype(F32) * 16.0 + jnp.sum(hot1 * (earlier + hot0), axis=0, keepdims=True)
+        line = iota((512, TOK), 0)
+        main_id = ((line >> 3) * 16 + (line & 7)).astype(F32)
+        rem_id = ((line >> 3) * 16 + 8 + (line & 1)).astype(F32)
+        e_main[...] = jnp.where((main_id == slot0) | (main_id == slot1), 1.0, 0.0).astype(BF)
+        e_rem[...] = jnp.where((rem_id == slot0) | (rem_id == slot1), 1.0, 0.0).astype(BF)
+        hosts = jnp.where(iota((EXPERTS, NREQ), 0) == placement_ref[...], 1.0, 0.0).astype(BF)
+        logits = logits_ref[...]
+        pick0 = jnp.sum(logits * dot(hosts, hot0.astype(BF)), axis=0, keepdims=True)
+        pick1 = jnp.sum(logits * dot(hosts, hot1.astype(BF)), axis=0, keepdims=True)
+        top = jnp.maximum(pick0, pick1)
+        exp0, exp1 = jnp.exp(pick0 - top), jnp.exp(pick1 - top)
+        total = exp0 + exp1
+        sub = iota((128, TOK), 0)
+        packed = jnp.where(sub == 0, slot0, jnp.where(sub == 1, slot1, jnp.where(sub == 2, exp0 / total, exp1 / total)))
+        turned = packed.T
+        s0, s1, w0, w1 = turned[:, 0:1], turned[:, 1:2], turned[:, 2:3], turned[:, 3:4]
+        col = iota((TOK, 512), 1)
+        for ids, ref in (((col >> 3) * 16 + (col & 7), g_main), ((col >> 3) * 16 + 8 + (col & 1), g_rem)):
+            ids = ids.astype(F32)
+            gate = jnp.where(ids == s0, w0, 0.0) + jnp.where(ids == s1, w1, 0.0)
+            high = gate.astype(BF)
+            ref[0] = high
+            ref[1] = (gate - high.astype(F32)).astype(BF)
+
+    for name, *at in PLAN:
+        if name == "heads":
+            heads()
+        elif name == "tables":
+            tables()
+        elif name == "R":
+            ring(*at)
+        elif name == "A":
+            need(*at)
+            attend(*at)
+        elif name == "z4":
+            send(0, 4, at[0], 1, 0)
+        elif name == "z8":
+            need(4, at[0])
+            send(4, 8, at[0], 1, 0)
+        elif name == "z6":
+            need(2, at[0])
+            send(2, 6, at[0], 1, 0)
+        elif name == "f":
+            along_x(1, 2, at[0], 1, (0, 2))
+            along_x(3, 2, at[0], 3, (1, 3))
+        else:
+            d, k = at
+            wrapped, second = int(name[1]), 4 * (name[2] == "b")
+            columns = tuple(v for v in ALL if (v in WRAPS[d]) == bool(wrapped))
+            along_x(4 * wrapped + second, d + second, k, d, columns)
 
     for k in range(2):
         out = acc[k] / mass[k]

time: 168 us -> 155 us (0.923); the launches traced: 168 us -> 153 us
  Pallas kernels: 167 us -> 152 us
    pallas_call x1, Pallas kernels: 167 us -> 152 us  [layer_call(): pl.pallas_call(layer_kernel, out_shape=jax.ShapeDtypeStruct((TOK, Q), BF)...]
where the time goes in v5:
time: 155 us; the launch traced here: 153 us
  Pallas kernels  152 us (98%)
  local copies, waits for them, and re-layouts  1.67 us (1%)
    pallas_call x1, Pallas kernels, layer_call(): pl.pallas_call(layer_kernel, out_shape=jax.ShapeDtypeStruct((TOK, Q), BF)...  152 us

profile of v5, /device:TPU:33, one launch (start us, length us, event | category | flops | bytes accessed | tf_op | source)
XLA Modules:
  0.0 153.4 jit_solution(10756950852859986189)
XLA Ops:
  0.0 151.7 %layer.1 = bf16[256,512]{1,0:T(8,128)(2,1)} custom-call(bf16[256,1024]{1,0:T(8,128)(2,1)} %q_hbm.1, bf16[256,512]{1,0:T(8,128)(2,1)} %k_hbm.1, bf16[256,512]{1,0:T(8,128)(2,1)} %v_hbm.1, s32[1,256]{1,0:T(1,128)} %bitcast.16, f32[8]{0:T(128)} %sink_ref.1, bf16[32,1024]{1,0:T(8,128)(2,1)} %bitcast.12, bf16[256,2048]{1,0:T(8,128)(2,1)} %res_hbm.1, ...), custom_call_target="tpu_custom_call" | custom-call | tf_op jit(solution)/shard_map/layer/pallas_call | solution.py:529
  151.7 1.7 %copy.16 = bf16[256,512]{1,0:T(8,128)(2,1)} copy(bf16[256,512]{1,0:T(8,128)(2,1)} %layer.1) | data formatting | bytes 524288

commit v6 on v5

--- a/solution.py
+++ b/solution.py
@@ -22,6 +22,10 @@
 Q = D // NFFN
 HID = 768
 WIDE = Q + 128
+PARTS = 4
+SPAN = 8 // PARTS
+LINES = 64 * SPAN
+TAIL = 16 * SPAN
 Z_ORDER = (0, 1, 7, 2, 6, 3, 5, 4)
 PLAN = (
     ("w0a", 1, 0), ("R", 0, 0), ("w0a", 3, 0), ("w0a", 3, 1), ("z4", 0), ("R", 1, 0), ("heads",), ("R", 0, 1),
@@ -413,23 +417,23 @@
     part2 = part.reshape(4, 512, WIDE)
     fin2 = fin.reshape(512, WIDE)
     from_l2, from_r2 = from_l.reshape(512, WIDE), from_r.reshape(512, WIDE)
-    hop_l2, hop_r2 = hop_l.reshape(2, 128, WIDE), hop_r.reshape(2, 128, WIDE)
-    row_id, line_id = iota((64, 256), 0), iota((64, 256), 1)
-    line_of, row_of = iota((256, 256), 0), iota((256, 256), 1)
+    hop_l2, hop_r2 = hop_l.reshape(PARTS, LINES // 2, WIDE), hop_r.reshape(PARTS, LINES // 2, WIDE)
+    row_id, line_id = iota((TAIL, LINES), 0), iota((TAIL, LINES), 1)
+    line_of, row_of = iota((LINES, LINES), 0), iota((LINES, LINES), 1)
     scatter = jnp.where(
-        line_of == ((row_of & 63) >> 1) * 8 + 2 * (row_of >> 6) + (row_of & 1), 1.0, 0.0
+        line_of == (row_of % TAIL >> 1) * 8 + 2 * (row_of // TAIL) + (row_of & 1), 1.0, 0.0
     ).astype(BF)
     rs = []
 
     def hidden_units(p):
-        starts_at = [pl.multiple_of(lax.rem(z + Z_ORDER[4 * p + j], NZ) * 64, 64) for j in range(4)]
+        starts_at = [pl.multiple_of(lax.rem(z + Z_ORDER[SPAN * p + j], NZ) * 64, 64) for j in range(SPAN)]
         for q in range(4):
-            for j in range(4):
+            for j in range(SPAN):
                 xbuf[64 * j:64 * j + 64, Q * q:Q * q + Q] = rows2[q, pl.ds(starts_at[j], 64), 0:Q]
             tails = jnp.concatenate([rows2[q, pl.ds(at, 64), Q:WIDE] for at in starts_at], axis=0)
             for k in range(4):
                 select = jnp.where(line_id == (row_id >> 1) * 8 + 2 * k + (row_id & 1), 1.0, 0.0).astype(BF)
-                xbuf[256:320, Q * q + 128 * k:Q * q + 128 * k + 128] = dot(select, tails).astype(BF)
+                xbuf[LINES:LINES + TAIL, Q * q + 128 * k:Q * q + 128 * k + 128] = dot(select, tails).astype(BF)
 
         def inner(n, carry):
             cols = pl.ds(pl.multiple_of(n * 256, 256), 256)
@@ -446,13 +450,13 @@
         rs.append(copy)
 
     def outputs(p):
-        low, high = pl.ds(32 * p, 16), pl.ds(32 * p + 16, 16)
+        low, high = pl.ds(8 * SPAN * p, 4 * SPAN), pl.ds(8 * SPAN * p + 4 * SPAN, 4 * SPAN)
         for j, which in enumerate((y2, yp, ym, y)):
             piece_out = dot_nt(act[...], wd[pl.ds(pl.multiple_of(which * Q, Q), Q), :])
-            part2[j, 256 * p:256 * p + 256, 0:Q] = piece_out[0:256].astype(BF)
-            tail = piece_out[256:320].astype(BF)
+            part2[j, LINES * p:LINES * p + LINES, 0:Q] = piece_out[0:LINES].astype(BF)
+            tail = piece_out[LINES:LINES + TAIL].astype(BF)
             stacked = jnp.concatenate([tail[:, 128 * k:128 * k + 128] for k in range(4)], axis=0)
-            part2[j, 256 * p:256 * p + 256, Q:WIDE] = dot(scatter, stacked).astype(BF)
+            part2[j, LINES * p:LINES * p + LINES, Q:WIDE] = dot(scatter, stacked).astype(BF)
             if j == 0:
                 reduce_send(p, 0, part.at[0, low], hop_l.at[p], yp)
                 reduce_send(p, 1, part.at[0, high], hop_r.at[p], ym)
@@ -462,8 +466,9 @@
                 reduce_send(p, 3, part.at[2, low], from_r.at[low], ym)
 
     def hop(p):
-        low, high = pl.ds(32 * p, 16), pl.ds(32 * p + 16, 16)
-        low2, high2 = slice(256 * p, 256 * p + 128), slice(256 * p + 128, 256 * p + 256)
+        low, high = pl.ds(8 * SPAN * p, 4 * SPAN), pl.ds(8 * SPAN * p + 4 * SPAN, 4 * SPAN)
+        middle = LINES * p + LINES // 2
+        low2, high2 = slice(LINES * p, middle), slice(middle, LINES * p + LINES)
         pltpu.make_async_copy(hop_l.at[p], hop_l.at[p], rs_rsem.at[p, 0]).wait()
         part2[1, low2, :] = (part2[1, low2, :].astype(F32) + hop_l2[p].astype(F32)).astype(BF)
         reduce_send(p, 4, part.at[1, low], from_l.at[low], yp)
@@ -472,31 +477,33 @@
         reduce_send(p, 5, part.at[2, high], from_r.at[high], ym)
 
     def give_back(p):
-        low, high = pl.ds(32 * p, 16), pl.ds(32 * p + 16, 16)
+        low, high = pl.ds(8 * SPAN * p, 4 * SPAN), pl.ds(8 * SPAN * p + 4 * SPAN, 4 * SPAN)
         for ref, half, k in ((from_l, high, 2), (from_r, low, 3), (from_l, low, 4), (from_r, high, 5)):
             view = ref.at[half]
             pltpu.make_async_copy(view, view, rs_rsem.at[p, k]).wait()
-        at = slice(256 * p, 256 * p + 256)
+        at = slice(LINES * p, LINES * p + LINES)
         total_out = part2[3, at, :].astype(F32) + from_l2[at, :].astype(F32) + from_r2[at, :].astype(F32)
         fin2[at, :] = total_out.astype(BF)
-        exchange(fin, ret, ret_ssem, ret_rsem, range(4 * p, 4 * p + 4), True)
-
-    for i in range(4):
-        gathered(i)
-    loads[2].wait()
-    loads[3].wait()
-    hidden_units(0)
-    forward(7)
-    loads[4].wait()
-    outputs(0)
-    for i in range(4, 8):
-        gathered(i)
-    hidden_units(1)
-    hop(0)
-    outputs(1)
-    give_back(0)
-    hop(1)
-    give_back(1)
+        exchange(fin, ret, ret_ssem, ret_rsem, range(SPAN * p, SPAN * p + SPAN), True)
+
+    for p in range(PARTS):
+        for i in range(SPAN * p, SPAN * p + SPAN):
+            gathered(i)
+        if p == 0:
+            loads[2].wait()
+            loads[3].wait()
+        hidden_units(p)
+        if p == 0:
+            forward(7)
+            loads[4].wait()
+        if p > 0:
+            hop(p - 1)
+        if p > 1:
+            give_back(p - 2)
+        outputs(p)
+    give_back(PARTS - 2)
+    hop(PARTS - 1)
+    give_back(PARTS - 1)
     for dz in Z_ORDER:
         arrived(ret, ret_rsem, dz)
     ret2 = ret.reshape(512, WIDE)
@@ -542,13 +549,13 @@
             pltpu.VMEM((8, TOK), F32), pltpu.VMEM((3, 8, TOK), F32),
             pltpu.VMEM((512, TOK), BF), pltpu.VMEM((512, TOK), BF),
             pltpu.VMEM((2, TOK, 512), BF), pltpu.VMEM((2, TOK, 512), BF),
-            pltpu.VMEM(chunk, BF), pltpu.VMEM((4,) + chunk, BF), pltpu.VMEM((320, D), BF), pltpu.VMEM((320, HID), BF),
-            pltpu.VMEM((4,) + chunk, BF), pltpu.VMEM((2, 16, 8, WIDE), BF), pltpu.VMEM((2, 16, 8, WIDE), BF),
+            pltpu.VMEM(chunk, BF), pltpu.VMEM((4,) + chunk, BF), pltpu.VMEM((LINES + TAIL, D), BF), pltpu.VMEM((LINES + TAIL, HID), BF),
+            pltpu.VMEM((4,) + chunk, BF), pltpu.VMEM((PARTS, 4 * SPAN, 8, WIDE), BF), pltpu.VMEM((PARTS, 4 * SPAN, 8, WIDE), BF),
             pltpu.VMEM(chunk, BF), pltpu.VMEM(chunk, BF), pltpu.VMEM(chunk, BF), pltpu.VMEM(chunk, BF),
             dma((9, 2)), dma((9, 2)), dma((9,)), dma((4,)), dma((5,)), dma((1,)), dma((1,)), dma((7, 2)), dma((7, 2)),
             dma, dma, dma, dma,
             dma((5,)), dma((3,)), dma((3,)), dma((3,)), dma((3,)),
-            dma, dma((8,)), dma((3, 8)), dma((3, 8)), dma((2, 6)), dma((2, 6)), dma, dma((8,)), dma,
+            dma, dma((8,)), dma((3, 8)), dma((3, 8)), dma((PARTS, 6)), dma((PARTS, 6)), dma, dma((8,)), dma,
         ],
         compiler_params=pltpu.CompilerParams(
             collective_id=1, has_side_effects=True, vmem_limit_bytes=60 << 20

time: 155 us -> 152 us (0.981)
  Pallas kernels: 152 us -> 150 us
    pallas_call x1, Pallas kernels: 152 us -> 150 us  [layer_call(): pl.pallas_call(layer_kernel, out_shape=jax.ShapeDtypeStruct((TOK, Q), BF)...]
where the time goes in v6:
time: 152 us
  Pallas kernels  150 us (99%)
  local copies, waits for them, and re-layouts  1.67 us (1%)
    pallas_call x1, Pallas kernels, layer_call(): pl.pallas_call(layer_kernel, out_shape=jax.ShapeDtypeStruct((TOK, Q), BF)...  150 us

profile of v6, /device:TPU:33, one launch (start us, length us, event | category | flops | bytes accessed | tf_op | source)
XLA Modules:
  0.0 151.6 jit_solution(16641320226769928543)
XLA Ops:
  0.0 149.9 %layer.1 = bf16[256,512]{1,0:T(8,128)(2,1)} custom-call(bf16[256,1024]{1,0:T(8,128)(2,1)} %q_hbm.1, bf16[256,512]{1,0:T(8,128)(2,1)} %k_hbm.1, bf16[256,512]{1,0:T(8,128)(2,1)} %v_hbm.1, s32[1,256]{1,0:T(1,128)} %bitcast.16, f32[8]{0:T(128)} %sink_ref.1, bf16[32,1024]{1,0:T(8,128)(2,1)} %bitcast.12, bf16[256,2048]{1,0:T(8,128)(2,1)} %res_hbm.1, ...), custom_call_target="tpu_custom_call" | custom-call | tf_op jit(solution)/shard_map/layer/pallas_call | solution.py:536
  150.0 1.7 %copy.16 = bf16[256,512]{1,0:T(8,128)(2,1)} copy(bf16[256,512]{1,0:T(8,128)(2,1)} %layer.1) | data formatting | bytes 524288

commit v7 on v6

--- a/solution.py
+++ b/solution.py
@@ -28,14 +28,14 @@
 TAIL = 16 * SPAN
 Z_ORDER = (0, 1, 7, 2, 6, 3, 5, 4)
 PLAN = (
-    ("w0a", 1, 0), ("R", 0, 0), ("w0a", 3, 0), ("w0a", 3, 1), ("z4", 0), ("R", 1, 0), ("heads",), ("R", 0, 1),
-    ("z4", 1), ("w0a", 1, 1), ("w1a", 3, 0), ("w1a", 1, 0), ("w0b", 1, 0), ("R", 2, 0), ("R", 1, 1),
-    ("w1a", 3, 1), ("f", 0), ("w1a", 1, 1), ("z8", 0), ("A", 1, 0), ("w0b", 3, 0), ("R", 2, 1), ("tables",),
-    ("A", 4, 1), ("z8", 1), ("R", 3, 0), ("R", 3, 1), ("A", 0, 1), ("f", 1), ("w1b", 1, 0), ("A", 8, 0),
-    ("A", 1, 1), ("R", 4, 0), ("R", 4, 1), ("A", 3, 0), ("w0b", 1, 1), ("z6", 0), ("A", 3, 1), ("w1b", 1, 1),
-    ("w1b", 3, 1), ("A", 0, 0), ("R", 5, 0), ("A", 2, 0), ("w1b", 3, 0), ("w0b", 3, 1), ("A", 2, 1),
-    ("R", 5, 1), ("z6", 1), ("A", 4, 0), ("A", 5, 0), ("R", 6, 0), ("A", 5, 1), ("A", 6, 0), ("R", 6, 1),
-    ("A", 8, 1), ("A", 6, 1), ("A", 7, 1), ("A", 7, 0), ("R", 7, 0), ("R", 7, 1),
+    ("z4", 0), ("w0a", 1, 0), ("w0a", 3, 0), ("R", 0, 0), ("R", 0, 1), ("R", 1, 0), ("z4", 1), ("w1a", 1, 0),
+    ("w1a", 3, 0), ("w0a", 3, 1), ("w0a", 1, 1), ("R", 1, 1), ("w1a", 3, 1), ("z8", 1), ("w0b", 1, 1),
+    ("R", 2, 1), ("w1a", 1, 1), ("heads",), ("R", 2, 0), ("A", 4, 1), ("f", 0), ("z8", 0), ("R", 3, 1),
+    ("A", 0, 1), ("R", 3, 0), ("tables",), ("A", 1, 0), ("w1b", 1, 1), ("w0b", 3, 0), ("R", 4, 1), ("f", 1),
+    ("A", 4, 0), ("A", 8, 0), ("R", 4, 0), ("A", 3, 1), ("w0b", 1, 0), ("z6", 0), ("w0b", 3, 1), ("w1b", 3, 0),
+    ("A", 2, 0), ("R", 5, 1), ("A", 0, 0), ("w1b", 1, 0), ("A", 5, 1), ("A", 8, 1), ("w1b", 3, 1), ("R", 5, 0),
+    ("z6", 1), ("A", 1, 1), ("A", 3, 0), ("R", 6, 1), ("A", 6, 0), ("A", 2, 1), ("R", 6, 0), ("A", 5, 0),
+    ("A", 7, 0), ("A", 6, 1), ("A", 7, 1), ("R", 7, 0), ("R", 7, 1),
 )
 ALL = (0, 1, 2, 3)
 WRAPS = {1: (3,), 3: (1, 2, 3)}

time: 152 us -> 151 us (level)
  no operation moved by 1% of the time
where the time goes in v7:
time: 151 us
  Pallas kernels  149 us (99%)
  local copies, waits for them, and re-layouts  1.67 us (1%)
    pallas_call x1, Pallas kernels, layer_call(): pl.pallas_call(layer_kernel, out_shape=jax.ShapeDtypeStruct((TOK, Q), BF)...  149 us

profile of v7, /device:TPU:33, one launch (start us, length us, event | category | flops | bytes accessed | tf_op | source)
XLA Modules:
  0.0 150.8 jit_solution(6588138857878066496)
XLA Ops:
  0.0 149.1 %layer.1 = bf16[256,512]{1,0:T(8,128)(2,1)} custom-call(bf16[256,1024]{1,0:T(8,128)(2,1)} %q_hbm.1, bf16[256,512]{1,0:T(8,128)(2,1)} %k_hbm.1, bf16[256,512]{1,0:T(8,128)(2,1)} %v_hbm.1, s32[1,256]{1,0:T(1,128)} %bitcast.16, f32[8]{0:T(128)} %sink_ref.1, bf16[32,1024]{1,0:T(8,128)(2,1)} %bitcast.12, bf16[256,2048]{1,0:T(8,128)(2,1)} %res_hbm.1, ...), custom_call_target="tpu_custom_call" | custom-call | tf_op jit(solution)/shard_map/layer/pallas_call | solution.py:536
  149.1 1.7 %copy.16 = bf16[256,512]{1,0:T(8,128)(2,1)} copy(bf16[256,512]{1,0:T(8,128)(2,1)} %layer.1) | data formatting | bytes 524288
